TPU v7x, 128 devices: a whole 4x4x4 slice. The times are simulated.
128 devices in a mesh: dp: 4 (over x), block: 32 (over z, y, core).
Axes of the slice: x: 4, y: 4, z: 4, core: 2. Of those that a mesh axis runs over, the one named last changes fastest.
Arguments:
- grad_partial: float32 [4, 4, 32, 512, 512], P('dp', None, None, 'block'), may hold values from -6 to 6
- owner_table: int32 [4, 32], replicated, may hold values from 0 to 31, as said below
- left_factor: float32 [4, 32, 2, 512, 512], P('dp', 'block'), as said below
- right_factor: float32 [4, 32, 2, 512, 512], P('dp', 'block'), as said below
Outputs:
- update: bfloat16 [4, 32, 512, 512], P('dp', None, 'block')
- left_out: float32 [4, 32, 2, 512, 512], P('dp', 'block')
- right_out: float32 [4, 32, 2, 512, 512], P('dp', 'block')
Inputs may be any that keep to these rules, and one draw needn't show every extreme that they name: owner_table[d, j] is the owner of block (d, j); within each row d no owner appears more than 2 times, and some owner appears exactly 2 times. `left_factor`: each slot holds a symmetric positive definite matrix. `right_factor`: each slot holds a symmetric positive definite matrix.
All inputs are finite; a program needn't handle non-finite values.
Results may differ from a plain program's by a relative error of at most 0.0072.
Values may be sent and summed in bfloat16 or wider, within the bound.
A program may use at most 128 MiB of HBM per device.

v0:
```python
import jax
import jax.numpy as jnp
from jax import lax
from jax.sharding import Mesh
from jax.sharding import PartitionSpec as P

MOST = 2
ITERS = 3
POWER = 8
BLOCK = ("block_0", "block_1", "block_2")


decay_rate = 0.9
damping = 0.1
epsilon = 1e-06


def split_up(x, dim, count):
    before, after = (x.shape[:dim], x.shape[dim + 1 :])
    return jnp.moveaxis(x.reshape(*before, count, -1, *after), dim, 0)


def sent_and_summed(x, axis, dim):
    parts = split_up(x, dim, lax.axis_size(axis))
    arrived = lax.all_to_all(parts, axis, split_axis=0, concat_axis=0, tiled=True)
    return arrived.sum(axis=0)


def in_order(parts, dim):
    lengths = list(parts.shape[1:])
    lengths[dim] *= parts.shape[0]
    return jnp.moveaxis(parts, 0, dim).reshape(lengths)


def exchange_in_order(parts, axes, order):
    lengths = [lax.axis_size(a) for a in axes]
    parts = parts.reshape(*lengths, *parts.shape[1:])
    for k in order:
        parts = lax.all_to_all(parts, axes[k], split_axis=k, concat_axis=k, tiled=True)
    return parts.reshape(-1, *parts.shape[len(axes) :])


def exchange_by_chip(x, groups, order, split_dim, concat_dim):
    count = lax.axis_size(groups[0]) * lax.axis_size(groups[1])
    parts = split_up(x, split_dim, count)
    return in_order(exchange_in_order(parts, groups, order), concat_dim)


def inverse_root(factor):
    size = factor.shape[0]
    identity = jnp.eye(size, dtype=jnp.float32)
    shifted = factor + damping * identity
    vector = jnp.ones((size,), jnp.float32) / jnp.sqrt(jnp.float32(size))
    length = jnp.float32(1.0)
    for iteration in range(POWER):
        product = jnp.dot(shifted, vector, precision=lax.Precision.HIGHEST)
        length = jnp.sqrt(jnp.sum(product * product))
        vector = product / length
    ceiling = 1.25 * length
    scaled = shifted / ceiling
    inverse = identity * ceiling ** (-0.25)
    for iteration in range(ITERS):
        step_matrix = (5.0 * identity - scaled) / 4.0
        inverse = jnp.dot(inverse, step_matrix, precision=lax.Precision.HIGHEST)
        square = jnp.dot(step_matrix, step_matrix, precision=lax.Precision.HIGHEST)
        fourth = jnp.dot(square, square, precision=lax.Precision.HIGHEST)
        scaled = jnp.dot(fourth, scaled, precision=lax.Precision.HIGHEST)
    return inverse


def precondition(gradient, left_state, right_state):
    size = gradient.shape[0]
    left_term = jnp.dot(gradient, gradient.T, preferred_element_type=jnp.float32) / size
    right_term = jnp.dot(gradient.T, gradient, preferred_element_type=jnp.float32) / size
    new_left = decay_rate * left_state + (1.0 - decay_rate) * left_term
    new_right = decay_rate * right_state + (1.0 - decay_rate) * right_term
    left_root = inverse_root(new_left).astype(jnp.bfloat16)
    right_root = inverse_root(new_right).astype(jnp.bfloat16)
    half = jnp.dot(left_root, gradient, preferred_element_type=jnp.float32).astype(jnp.bfloat16)
    shaped = jnp.dot(half, right_root, preferred_element_type=jnp.float32)
    gradient_wide = gradient.astype(jnp.float32)
    graft_scale = jnp.sqrt(jnp.mean(gradient_wide * gradient_wide)) / jnp.sqrt(
        jnp.mean(shaped * shaped) + epsilon
    )
    return ((shaped * graft_scale).astype(jnp.bfloat16), new_left, new_right)


def slot_chooser(table_row, count):
    order = jnp.arange(count, dtype=jnp.int32)
    earlier = order[:, None] < order[None, :]
    matching = table_row[:, None] == table_row[None, :]
    slot_rank = jnp.sum(jnp.logical_and(matching, earlier), axis=0)
    owner_ids = jnp.repeat(order, MOST)
    slot_ids = jnp.tile(jnp.arange(MOST, dtype=jnp.int32), count)
    return jnp.logical_and(
        table_row[None, :] == owner_ids[:, None], slot_rank[None, :] == slot_ids[:, None]
    )


def local(grad_partial, owner_table, left_factor, right_factor):
    count = grad_partial.shape[2]
    stripe = grad_partial.shape[3]
    size = grad_partial.shape[4]
    data_index = lax.axis_index("dp")
    owner_index = lax.axis_index(BLOCK)
    table_row = lax.dynamic_index_in_dim(owner_table, data_index, 0, keepdims=False)
    chooser = slot_chooser(table_row, count)
    weights = chooser.astype(jnp.bfloat16)
    summed = sent_and_summed(grad_partial[0], "dp", 0)
    stripes = summed[0].astype(jnp.bfloat16).reshape(count, stripe * size)
    outgoing = jnp.dot(weights, stripes, preferred_element_type=jnp.float32)
    outgoing = outgoing.astype(jnp.bfloat16).reshape(count, MOST, stripe, size)
    received = lax.all_to_all(outgoing, BLOCK, split_axis=0, concat_axis=2, tiled=True)
    own_slots = lax.dynamic_slice_in_dim(chooser, owner_index * MOST, MOST, 0)
    active = jnp.any(own_slots, axis=1)
    updates = []
    new_lefts = []
    new_rights = []
    for slot in range(MOST):
        result, new_left, new_right = precondition(
            received[0, slot], left_factor[0, 0, slot], right_factor[0, 0, slot]
        )
        updates.append(result)
        new_lefts.append(jnp.where(active[slot], new_left, left_factor[0, 0, slot]))
        new_rights.append(jnp.where(active[slot], new_right, right_factor[0, 0, slot]))
    returning = jnp.stack(updates).reshape(MOST, count, stripe, size)
    returned = exchange_by_chip(returning, (("block_0", "block_1"), "block_2"), (0, 1), 1, 0)
    placed = jnp.dot(
        weights.T, returned.reshape(count * MOST, stripe * size), preferred_element_type=jnp.float32
    )
    placed = placed.astype(jnp.bfloat16).reshape(1, count, stripe, size)
    return (placed, jnp.stack(new_lefts)[None, None], jnp.stack(new_rights)[None, None])


def solution(mesh):
    torus = Mesh(
        mesh.devices.reshape(mesh.shape["dp"], 4, 4, 2), ("dp", "block_0", "block_1", "block_2")
    )
    placed = (
        P("dp", None, None, BLOCK, None),
        P(),
        P("dp", BLOCK, None, None, None),
        P("dp", BLOCK, None, None, None),
    )
    return jax.shard_map(
        local,
        mesh=torus,
        in_specs=placed,
        out_specs=(
            P("dp", None, BLOCK, None),
            P("dp", BLOCK, None, None, None),
            P("dp", BLOCK, None, None, None),
        ),
        check_vma=False,
    )
```

profile of v0, /device:TPU:1, one launch (start us, length us, event | category | flops | bytes accessed | tf_op | source)
XLA Modules:
  0.0 305.8 jit_solution(6805516658287558514)
XLA Ops:
  0.6 4.9 %all-to-all-start = ((f32[4,1,32,16,512]{4,3,2,1,0:T(8,128)}), f32[4,1,32,16,512]{4,3,2,1,0:T(8,128)}, u32[]{:S(2)}, u32[]{:S(2)}) async-start(f32[4,1,32,16,512]{4,3,2,1,0:T(8,128)} %bitcast.228), calls=%async_computation | async-start | bytes 8388608 | tf_op jit(solution)/shard_map/all_to_all | solution.py:25
  5.9 48.4 %all-to-all-done = f32[4,1,32,16,512]{4,3,2,1,0:T(8,128)} async-done(((f32[4,1,32,16,512]{4,3,2,1,0:T(8,128)}), f32[4,1,32,16,512]{4,3,2,1,0:T(8,128)}, u32[]{:S(2)}, u32[]{:S(2)}) %all-to-all-start) | async-done | bytes 4194336 | tf_op jit(solution)/shard_map/all_to_all | solution.py:25
  54.2 2.7 reduce_sum.343
  58.1 27.1 %all_to_all.33 = bf16[32,2,16,512]{3,2,1,0:T(8,128)(2,1)S(1)} all-to-all(bf16[32,2,16,512]{3,2,1,0:T(8,128)(2,1)S(1)} %bitcast.232), channel_id=1, replica_groups=mesh['dp'=4,'block_0'=4,'block_1'=4,'block_2'=2] {'block_0','block_1','b..., dimensions={0} | all-to-all | bytes 2097152 | tf_op jit(solution)/shard_map/all_to_all | solution.py:113
  104.6 3.0 fusion.55
  128.2 3.0 fusion.48
  132.2 2.0 fusion.1
  152.9 3.4 %fusion.41 = f32[512,512]{1,0:T(8,128)} fusion(f32[]{:T(128)S(6)} %mul.282, f32[512,512]{1,0:T(8,128)S(1)} %fusion.1), kind=kOutput, calls=%fused_computation.81 | convolution fusion | flops 1612447744 | bytes 2097156 | tf_op jit(solution)/shard_map/dot_general | solution.py:65
  156.4 2.0 fusion
  161.7 2.2 fusion.202
  165.3 2.2 fusion.201
  168.9 2.2 fusion.200
  172.4 2.2 fusion.199
  176.0 2.2 fusion.198
  179.5 2.2 fusion.197
  183.1 2.2 fusion.196
  186.6 4.6 %fusion.34 = f32[512,512]{1,0:T(8,128)} fusion(f32[]{:T(128)S(6)} %mul.295, f32[512,512]{1,0:T(8,128)} %copy-done.2), kind=kOutput, calls=%fused_computation.78 | convolution fusion | flops 1612447744 | bytes 2097156 | tf_op jit(solution)/shard_map/dot_general | solution.py:65
  191.3 3.4 %fusion.204 = f32[512,512]{1,0:T(8,128)S(1)} fusion(f32[512,512]{1,0:T(8,128)} %fusion.55), kind=kOutput, calls=%fused_computation.305 | convolution fusion | flops 1610612736 | bytes 2097152 | tf_op jit(solution)/shard_map/dot_general | solution.py:66
  194.7 2.1 fusion.171
  196.8 1.9 fusion.51
  200.6 1.8 fusion.4
  202.4 1.9 fusion.28
  204.4 1.9 fusion.53
  208.1 2.1 fusion.172
  210.3 1.9 fusion.44
  215.9 1.9 fusion.26
  217.8 1.9 fusion.46
  219.7 2.6 convolution_convert_fusion.7
  222.4 3.1 %convolution_convert_fusion.6 = bf16[512,512]{1,0:T(8,128)(2,1)} fusion(f32[512,512]{1,0:T(8,128)S(1)} %fusion.46, f32[512,512]{1,0:T(8,128)S(1)} %fusion.5), kind=kOutput, calls=%fused_computation.36 | convolution fusion | flops 1610874880 | bytes 2621440 | tf_op jit(solution)/shard_map/dot_general | solution.py:64
  225.4 3.7 %multiply_reduce_fusion.2 = (f32[]{:T(128)}, f32[512,512]{1,0:T(8,128)}) fusion(bf16[512,512]{1,0:T(8,128)(2,1)} %convolution_convert_fusion.6, bf16[512,512]{1,0:T(8,128)(2,1)} %convolution_convert_fusion.7, bf16[1,2,512,512]{3,2,1,0:T(8,128)(2,1)} %bitcast.226), kind=kOutput, calls=%fused_computation.69 | convolution fusion | flops 537657344 | bytes 2621444 | tf_op jit(solution)/shard_map/dot_general | solution.py:80
  230.3 3.4 %fusion.208 = f32[512,512]{1,0:T(8,128)S(1)} fusion(f32[512,512]{1,0:T(8,128)} %fusion.41), kind=kOutput, calls=%fused_computation.309 | convolution fusion | flops 1610612736 | bytes 2097152 | tf_op jit(solution)/shard_map/dot_general | solution.py:66
  233.7 1.9 fusion.173
  235.6 1.9 fusion.37
  239.4 1.9 fusion.6
  241.3 1.9 fusion.24
  243.2 2.1 fusion.39
  247.2 1.9 fusion.174
  249.1 1.9 fusion.30
  254.7 1.9 fusion.22
  256.6 2.1 fusion.32
  258.8 2.6 convolution_convert_fusion.5
  261.4 2.6 convolution_convert_fusion.4
  264.1 3.7 %multiply_reduce_fusion = (f32[]{:T(128)}, f32[512,512]{1,0:T(8,128)}) fusion(bf16[512,512]{1,0:T(8,128)(2,1)} %convolution_convert_fusion.4, bf16[512,512]{1,0:T(8,128)(2,1)} %convolution_convert_fusion.5, bf16[1,2,512,512]{3,2,1,0:T(8,128)(2,1)} %bitcast.227), kind=kOutput, calls=%fused_computation.62 | convolution fusion | flops 537657344 | bytes 2621444 | tf_op jit(solution)/shard_map/dot_general | solution.py:80
  269.1 2.1 multiply_convert_fusion.1
  274.8 4.3 %all-to-all-start.2 = ((bf16[16,2,2,1,16,512]{5,4,2,1,3,0:T(8,128)(2,1)}), bf16[16,2,2,1,16,512]{5,4,2,1,3,0:T(8,128)(2,1)}, u32[]{:S(2)}, u32[]{:S(2)}) async-start(bf16[16,2,2,1,16,512]{5,4,2,1,3,0:T(8,128)(2,1)} %bitcast.229), calls=%async_computation.2 | async-start | bytes 2097152 | tf_op jit(solution)/shard_map/all_to_all | solution.py:39
  280.0 4.8 %fusion.20 = (f32[1,512,512]{2,1,0:T(8,128)S(1)}, f32[1,512,512]{2,1,0:T(8,128)S(1)}, f32[1,512,512]{2,1,0:T(8,128)S(1)}, f32[1,512,512]{2,1,0:T(8,128)S(1)}) fusion(f32[512,512]{1,0:T(8,128)S(1)} %fusion.2, f32[1,1,2,512,512]{4,3,2,1,0:T(8,128)} %param.7, pred[]{:T(512)} %bitcast.77, f32[512,512]{1,0:T(8,128)} %copy-done.2, pred[]{:T(512)} %bitcast.79, ...), kind=kLoop, calls=%fused_computation.57 | loop fusion | flops 1048576 | bytes 12582914 | tf_op jit(solution)/shard_map/stack | solution.py:132
  287.8 8.3 %all-to-all-done.2 = bf16[16,2,2,1,16,512]{5,4,2,1,3,0:T(8,128)(2,1)} async-done(((bf16[16,2,2,1,16,512]{5,4,2,1,3,0:T(8,128)(2,1)}), bf16[16,2,2,1,16,512]{5,4,2,1,3,0:T(8,128)(2,1)}, u32[]{:S(2)}, u32[]{:S(2)}) %all-to-all-start.2) | async-done | bytes 1048608 | tf_op jit(solution)/shard_map/all_to_all | solution.py:39
  297.4 6.0 %all_to_all.34 = bf16[16,2,2,1,16,512]{5,4,2,0,3,1:T(8,128)(2,1)S(1)} all-to-all(bf16[16,2,2,1,16,512]{5,4,2,0,3,1:T(8,128)(2,1)S(1)} %copy.15), channel_id=1, replica_groups=mesh['dp'=4,'block_0'=4,'block_1'=4,'block_2'=2] {'block_2'}, dimensions={1} | all-to-all | bytes 2097152 | tf_op jit(solution)/shard_map/all_to_all | solution.py:39
  (135 shorter events, 76.7 us)
Async XLA Ops:
  0.6 5.1 %copy-start = (s32[4,32]{1,0:T(4,128)S(1)}, s32[4,32]{1,0:T(4,128)}, u32[]{:S(2)}) copy-start(s32[4,32]{1,0:T(4,128)} %param.5) | copy-start | bytes 1540
  0.6 53.6 %all-to-all-start = ((f32[4,1,32,16,512]{4,3,2,1,0:T(8,128)}), f32[4,1,32,16,512]{4,3,2,1,0:T(8,128)}, u32[]{:S(2)}, u32[]{:S(2)}) async-start(f32[4,1,32,16,512]{4,3,2,1,0:T(8,128)} %bitcast.228), calls=%async_computation | async-start | bytes 8388608 | tf_op jit(solution)/shard_map/all_to_all | solution.py:25
  58.1 27.3 %copy-start.5 = (f32[1,1,2,512,512]{4,3,2,1,0:T(8,128)S(1)}, f32[1,1,2,512,512]{4,3,2,1,0:T(8,128)}, u32[]{:S(2)}) copy-start(f32[1,1,2,512,512]{4,3,2,1,0:T(8,128)} %param.6) | copy-start | bytes 6291460
  85.4 45.9 %copy-start.4 = (bf16[32,2,16,512]{3,2,0,1:T(8,128)(2,1)}, bf16[32,2,16,512]{3,2,0,1:T(8,128)(2,1)S(1)}, u32[]{:S(2)}) copy-start(bf16[32,2,16,512]{3,2,0,1:T(8,128)(2,1)S(1)} %copy.13) | copy-start | bytes 3145732
  158.4 1.0 copy-start.2
  204.4 1.9 copy-start.6
  243.2 2.1 copy-start.7
  245.3 1.9 copy-start.3
  274.8 21.2 %all-to-all-start.2 = ((bf16[16,2,2,1,16,512]{5,4,2,1,3,0:T(8,128)(2,1)}), bf16[16,2,2,1,16,512]{5,4,2,1,3,0:T(8,128)(2,1)}, u32[]{:S(2)}, u32[]{:S(2)}) async-start(bf16[16,2,2,1,16,512]{5,4,2,1,3,0:T(8,128)(2,1)} %bitcast.229), calls=%async_computation.2 | async-start | bytes 2097152 | tf_op jit(solution)/shard_map/all_to_all | solution.py:39
  303.6 2.0 copy-start.1
where the time goes:
time: 310 us; the launch traced here: 306 us
  matrix products  137 us (44%)
  waiting for transfers between devices  56.7 us (18%)
  other arithmetic  36.3 us (12%)
  blocking collectives  33.2 us (11%)
  between operations  26.6 us (9%)
  starting transfers between devices  9.21 us (3%)
  local copies, waits for them, and re-layouts  6.66 us (2%)
    all_to_all x1, waiting for transfers between devices, sent_and_summed(): lax.all_to_all(parts, axis, split_axis=0, concat_axis=0, tiled=True)  48.4 us
    dot_general x32, matrix products, inverse_root(): product = jnp.dot(shifted, vector, precision=lax.Precision.HIGHEST)  41.2 us
    all_to_all x1, blocking collectives, local(): lax.all_to_all(outgoing, BLOCK, split_axis=0, concat_axis=2, tiled=True)  27.1 us
    dot_general x12, matrix products, inverse_root(): inverse = jnp.dot(inverse, step_matrix, precision=lax.Precision.HIGHEST)  26.7 us
    dot_general x8, matrix products, inverse_root(): square = jnp.dot(step_matrix, step_matrix, precision=lax.Precision.HIGHEST)  21.7 us
    reduce_sum x32, other arithmetic, inverse_root(): length = jnp.sqrt(jnp.sum(product * product))  19.8 us
    dot_general x8, matrix products, inverse_root(): fourth = jnp.dot(square, square, precision=lax.Precision.HIGHEST)  17.8 us
    dot_general x8, matrix products, inverse_root(): scaled = jnp.dot(fourth, scaled, precision=lax.Precision.HIGHEST)  15.4 us
  transfers between devices with their start and end apart: 2, of which 2 were waited for; matrix products, arithmetic and copies ran while one was open for 3% of the time, Pallas kernels for 0%

commit v1 on v0

v1 whole, which is shorter than its diff:
```python
import functools

import jax
import jax.numpy as jnp
from jax import lax
from jax.experimental import pallas as pl
from jax.experimental.pallas import tpu as pltpu
from jax.sharding import PartitionSpec as P

MOST = 2
POWER = 8
MESH = pl.DeviceIdType.MESH
F32 = jnp.float32
BF16 = jnp.bfloat16
MIB = 1 << 20

decay_rate = 0.9
damping = 0.1
epsilon = 1e-06

A1, A2, A3, A4, A5 = 625 / 256, -500 / 256, 150 / 256, -20 / 256, 1 / 256
R0 = 25 / 16
R1 = (-5 - 3125 / 256) / 16
R2 = 3125 / 256 / 16
R3 = -1250 / 256 / 16
R4 = 250 / 256 / 16
R5 = -25 / 256 / 16
R6 = 1 / 256 / 16


def dot(a, b):
    return jnp.dot(a, b, preferred_element_type=F32)


def gather_kernel(
    n_dp, count, lanes, table, grads, out, stage, raw, raw_in, cross, cross_in, both, both_in, summed,
    outgoing, load_sem, x_send, x_recv, o_send, o_recv,
):
    row, me = lax.axis_index("dp"), lax.axis_index("block")
    stripe = grads.shape[3]
    half = count // 2
    chunks = grads.shape[4] // lanes
    right, left, far = lax.rem(row + 1, n_dp), lax.rem(row + n_dp - 1, n_dp), lax.rem(row + 2, n_dp)

    barrier = pltpu.get_barrier_semaphore()
    for peer in (right, left):
        pl.semaphore_signal(barrier, inc=1, device_id=(peer, me), device_id_type=MESH)

    def greet(k, carry):
        pl.semaphore_signal(
            barrier, inc=1, device_id=(row, lax.rem(me + k, count)), device_id_type=MESH
        )
        return carry

    loads = []
    for n, d in enumerate((far, right, left, row)):
        load = pltpu.make_async_copy(grads.at[0, d], stage.at[n], load_sem.at[n])
        load.start()
        loads.append(load)
    lax.fori_loop(1, count, greet, 0)

    own_rows = pl.ds(pl.multiple_of(me * stripe, stripe), stripe)
    halves = (pl.ds(0, half), pl.ds(half, half))
    towards = (right, left)

    def cut(n, part, c):
        return stage[n, halves[part], :, pl.ds(c * lanes, lanes)]

    def x_copy(kind, way, c, src, dst):
        return pltpu.make_async_remote_copy(
            src_ref=src.at[way, c],
            dst_ref=dst.at[way, c],
            send_sem=x_send.at[kind, way, c],
            recv_sem=x_recv.at[kind, way, c],
            device_id=(towards[way], me),
            device_id_type=MESH,
        )

    loads[0].wait()
    for c in range(chunks):
        for way in range(2):
            raw[way, c] = cut(0, way, c).astype(BF16)
    loads[1].wait()
    loads[2].wait()
    for c in range(chunks):
        for way in range(2):
            cross[way, c] = cut(1 + way, 1 - way, c).astype(BF16)
    pl.semaphore_wait(barrier, count + 1)

    raws = [[x_copy(0, way, c, raw, raw_in) for way in range(2)] for c in range(chunks)]
    crosses = [[x_copy(1, way, c, cross, cross_in) for way in range(2)] for c in range(chunks)]
    boths = [[x_copy(2, way, c, both, both_in) for way in range(2)] for c in range(chunks)]

    def dispatch(c):
        columns = pl.ds(c * lanes, lanes)
        for way in range(2):
            crosses[c][way].wait_recv()
            boths[c][way].wait_recv()
        for part in range(2):
            total = cut(3, part, c) + both_in[part, c].astype(F32) + cross_in[1 - part, c].astype(F32)
            summed[c, halves[part]] = total.astype(BF16)

        def choose(o, carry):
            for s in range(MOST):
                outgoing[c, o, s] = summed[c, table[o * MOST + s]]
            return carry

        lax.fori_loop(0, count, choose, 0)

        def send(k, carry):
            o = lax.rem(me + k, count)
            pltpu.make_async_remote_copy(
                src_ref=outgoing.at[c, o],
                dst_ref=out.at[:, own_rows, columns],
                send_sem=o_send.at[c],
                recv_sem=o_recv.at[c],
                device_id=(row, o),
                device_id_type=MESH,
            ).start()
            return carry

        lax.fori_loop(1, count, send, 0)
        out[:, own_rows, columns] = outgoing[c, me]

    for way in range(2):
        raws[0][way].start()
    for c in range(chunks):
        if c + 1 < chunks:
            for way in range(2):
                raws[c + 1][way].start()
        for way in range(2):
            crosses[c][way].start()
        for way in range(2):
            raws[c][way].wait_recv()
            both[way, c] = (cut(1 + way, way, c) + raw_in[way, c].astype(F32)).astype(BF16)
            boths[c][way].start()
        if c == 0:
            loads[3].wait()
        if c > 0:
            dispatch(c - 1)
    dispatch(chunks - 1)

    for c in range(chunks):
        for way in range(2):
            raws[c][way].wait_send()
            crosses[c][way].wait_send()
            boths[c][way].wait_send()
    for c in range(chunks):
        arrived = outgoing.at[c, pl.ds(0, count - 1)]
        pltpu.make_async_copy(arrived, arrived, o_send.at[c]).wait()
        pltpu.make_async_copy(arrived, arrived, o_recv.at[c]).wait()


def gather_blocks(grads, table, n_dp, lanes):
    _, _, count, stripe, size = grads.shape
    chunks = size // lanes
    part = pltpu.VMEM((2, chunks, count // 2, stripe, lanes), BF16)
    return pl.pallas_call(
        functools.partial(gather_kernel, n_dp, count, lanes),
        name="gather_blocks",
        out_shape=jax.ShapeDtypeStruct((MOST, count * stripe, size), BF16),
        in_specs=[pl.BlockSpec(memory_space=pltpu.SMEM), pl.BlockSpec(memory_space=pl.ANY)],
        out_specs=pl.BlockSpec(memory_space=pltpu.VMEM),
        scratch_shapes=[
            pltpu.VMEM((4, count, stripe, size), F32),
            part, part, part, part, part, part,
            pltpu.VMEM((chunks, count, stripe, lanes), BF16),
            pltpu.VMEM((chunks, count, MOST, stripe, lanes), BF16),
            pltpu.SemaphoreType.DMA((4,)),
            pltpu.SemaphoreType.DMA((3, 2, chunks)),
            pltpu.SemaphoreType.DMA((3, 2, chunks)),
            pltpu.SemaphoreType.DMA((chunks,)),
            pltpu.SemaphoreType.DMA((chunks,)),
        ],
        compiler_params=pltpu.CompilerParams(
            collective_id=0, has_side_effects=True, vmem_limit_bytes=24 * MIB
        ),
    )(table, grads)


def diagonal(first, rows, size, value):
    down = lax.broadcasted_iota(jnp.int32, (rows, size), 0) + first
    across = lax.broadcasted_iota(jnp.int32, (rows, size), 1)
    return jnp.where(down == across, F32(value), F32(0))


def block_kernel(
    tall, active, blocks, left, right, left_out, right_out, result, flipped, factor, fresh, wide, wide2,
    m, u, v, w, load_sem, store_sem,
):
    size = blocks.shape[-1]
    chains = range(2 * MOST)
    tiles = [(i, pl.ds(i, tall)) for i in range(0, size, tall)]
    loads, stores = [], []
    for k in chains:
        slot, side = divmod(k, 2)
        load = pltpu.make_async_copy((left, right)[side].at[0, 0, slot], factor.at[k], load_sem.at[k])
        load.start()
        loads.append(load)
    for slot in range(MOST):
        flipped[slot] = blocks[slot].T

    def each(ks, step):
        for k in ks:
            for i, rows in tiles:
                step(k, i, rows)

    def gram(k, i, rows):
        slot, side = divmod(k, 2)
        first, second = (blocks, flipped) if side == 0 else (flipped, blocks)
        old = factor[k, rows, :]
        new = decay_rate * old + ((1.0 - decay_rate) / size) * dot(first[slot, rows, :], second[slot])
        fresh[k, rows, :] = jnp.where(active[slot] > 0, new, old)
        shifted = new + diagonal(i, tall, size, damping)
        wide[k, rows, :] = shifted
        m[k, rows, :] = shifted.astype(BF16)

    def roots(ks):
        for k in ks:
            loads[k].wait()
        each(ks, gram)
        for k in ks:
            slot, side = divmod(k, 2)
            store = pltpu.make_async_copy(
                fresh.at[k], (left_out, right_out)[side].at[0, 0, slot], store_sem.at[k]
            )
            store.start()
            stores.append(store)
        vector = {k: jnp.full((1, size), 1.0 / size**0.5, F32) for k in ks}
        length = {}
        for _ in range(POWER):
            for k in ks:
                high = vector[k].astype(BF16)
                low = (vector[k] - high.astype(F32)).astype(BF16)
                both = dot(jnp.concatenate([high, low], axis=0), m[k])
                product = both[0:1] + both[1:2]
                length[k] = jnp.sqrt(jnp.sum(product * product, axis=1, keepdims=True))
                vector[k] = product / length[k]
        ceiling = {k: 1.25 * length[k] for k in ks}
        inverse = {k: 1.0 / ceiling[k] for k in ks}
        scale = {k: lax.rsqrt(jnp.sqrt(ceiling[k])) for k in ks}

        def scaled(k, i, rows):
            value = wide[k, rows, :] * inverse[k]
            wide[k, rows, :] = value
            m[k, rows, :] = value.astype(BF16)

        def square(k, i, rows):
            product, value = dot(m[k, rows, :], m[k]), wide[k, rows, :]
            u[k, rows, :] = product.astype(BF16)
            wide[k, rows, :] = A1 * value + A2 * product
            v[k, rows, :] = (A4 * value + A5 * product).astype(BF16)

        def cube(k, i, rows):
            product = dot(m[k, rows, :], u[k])
            w[k, rows, :] = product.astype(BF16)
            wide[k, rows, :] += A3 * product

        def second(k, i, rows):
            value = wide[k, rows, :] + dot(w[k, rows, :], v[k])
            wide[k, rows, :] = value
            u[k, rows, :] = value.astype(BF16)

        def square_again(k, i, rows):
            product, value = dot(u[k, rows, :], u[k]), wide[k, rows, :]
            w[k, rows, :] = product.astype(BF16)
            wide[k, rows, :] = R1 * value + R2 * product
            wide2[k, rows, :] = R4 * value + R5 * product

        def cube_again(k, i, rows):
            product = dot(u[k, rows, :], w[k])
            wide[k, rows, :] += R3 * product
            v[k, rows, :] = (wide2[k, rows, :] + R6 * product).astype(BF16)
            wide2[k, rows, :] = product

        def tail(k, i, rows):
            value = wide[k, rows, :] + dot(wide2[k, rows, :].astype(BF16), v[k])
            value = value + diagonal(i, tall, size, R0)
            wide[k, rows, :] = value
            u[k, rows, :] = value.astype(BF16)

        def root(k, i, rows):
            value = 1.25 * wide[k, rows, :] - 0.25 * dot(m[k, rows, :], u[k])
            w[k, rows, :] = (value * scale[k]).astype(BF16)

        for step in (scaled, square, cube, second, square_again, cube_again, tail, root):
            each(ks, step)

    def shape_block(slot):
        one, two = 2 * slot, 2 * slot + 1
        for i, rows in tiles:
            u[one, rows, :] = dot(w[one, rows, :], blocks[slot]).astype(BF16)
        energy, power = jnp.zeros((1, size), F32), jnp.zeros((1, size), F32)
        for i, rows in tiles:
            shaped = dot(u[one, rows, :], w[two])
            wide[one, rows, :] = shaped
            original = blocks[slot, rows, :].astype(F32)
            energy += jnp.sum(shaped * shaped, axis=0, keepdims=True)
            power += jnp.sum(original * original, axis=0, keepdims=True)
        energy = jnp.sum(energy, axis=1, keepdims=True) / (size * size)
        power = jnp.sum(power, axis=1, keepdims=True) / (size * size)
        graft = jnp.sqrt(power) / jnp.sqrt(energy + epsilon)
        for i, rows in tiles:
            result[slot, rows, :] = (wide[one, rows, :] * graft).astype(BF16)

    roots(chains)
    for slot in range(MOST):
        shape_block(slot)
    for store in stores:
        store.wait()


def precondition(active, blocks, left, right, tall):
    size = blocks.shape[-1]
    wide = pltpu.VMEM((2 * MOST, size, size), F32)
    thin = pltpu.VMEM((2 * MOST, size, size), BF16)
    any_spec = pl.BlockSpec(memory_space=pl.ANY)
    vmem_spec = pl.BlockSpec(memory_space=pltpu.VMEM)
    return pl.pallas_call(
        functools.partial(block_kernel, tall),
        name="precondition",
        out_shape=(
            jax.ShapeDtypeStruct(left.shape, F32),
            jax.ShapeDtypeStruct(right.shape, F32),
            jax.ShapeDtypeStruct(blocks.shape, BF16),
        ),
        in_specs=[pl.BlockSpec(memory_space=pltpu.SMEM), vmem_spec, any_spec, any_spec],
        out_specs=(any_spec, any_spec, vmem_spec),
        scratch_shapes=[
            pltpu.VMEM((MOST, size, size), BF16),
            wide, wide, wide, wide, thin, thin, thin, thin,
            pltpu.SemaphoreType.DMA((2 * MOST,)),
            pltpu.SemaphoreType.DMA((2 * MOST,)),
        ],
        compiler_params=pltpu.CompilerParams(vmem_limit_bytes=48 * MIB),
    )(active, blocks, left, right)


def return_kernel(count, place, ready, update, back, send_sem, recv_sem):
    row, me = lax.axis_index("dp"), lax.axis_index("block")
    stripe = update.shape[1]
    barrier = pltpu.get_barrier_semaphore()

    def greet(k, carry):
        pl.semaphore_signal(
            barrier, inc=1, device_id=(row, lax.rem(me + k, count)), device_id_type=MESH
        )
        return carry

    lax.fori_loop(1, count, greet, 0)
    pl.semaphore_wait(barrier, count - 1)

    def send(k, carry):
        o = lax.rem(me + k, count)
        pltpu.make_async_remote_copy(
            src_ref=ready.at[:, pl.ds(pl.multiple_of(o * stripe, stripe), stripe), :],
            dst_ref=back.at[pl.ds(me * MOST, MOST)],
            send_sem=send_sem,
            recv_sem=recv_sem,
            device_id=(row, o),
            device_id_type=MESH,
        ).start()
        return carry

    lax.fori_loop(1, count, send, 0)
    back[pl.ds(me * MOST, MOST)] = ready[:, pl.ds(pl.multiple_of(me * stripe, stripe), stripe), :]
    arrived = back.at[pl.ds(0, MOST * (count - 1))]
    pltpu.make_async_copy(arrived, arrived, send_sem).wait()
    pltpu.make_async_copy(arrived, arrived, recv_sem).wait()

    def put(j, carry):
        update[j] = back[place[j]]
        return carry

    lax.fori_loop(0, count, put, 0)


def return_blocks(ready, place, count):
    _, rows, size = ready.shape
    vmem_spec = pl.BlockSpec(memory_space=pltpu.VMEM)
    stripe = rows // count
    return pl.pallas_call(
        functools.partial(return_kernel, count),
        name="return_blocks",
        out_shape=jax.ShapeDtypeStruct((count, stripe, size), BF16),
        in_specs=[pl.BlockSpec(memory_space=pltpu.SMEM), vmem_spec],
        out_specs=vmem_spec,
        scratch_shapes=[
            pltpu.VMEM((MOST * count, stripe, size), BF16),
            pltpu.SemaphoreType.DMA,
            pltpu.SemaphoreType.DMA,
        ],
        compiler_params=pltpu.CompilerParams(
            collective_id=1, has_side_effects=True, vmem_limit_bytes=16 * MIB
        ),
    )(place, ready)


def tables(owners):
    count = owners.shape[0]
    order = jnp.arange(count, dtype=jnp.int32)
    same = owners[:, None] == owners[None, :]
    rank = jnp.sum(same & (order[:, None] < order[None, :]), axis=0, dtype=jnp.int32)
    place = owners * MOST + rank
    slots = jnp.arange(MOST * count, dtype=jnp.int32)
    holds = place[None, :] == slots[:, None]
    block_of = jnp.sum(jnp.where(holds, order[None, :], 0), axis=1, dtype=jnp.int32)
    return place, block_of, jnp.any(holds, axis=1).astype(jnp.int32)


def local(n_dp, grad_partial, owner_table, left_factor, right_factor):
    row, me = lax.axis_index("dp"), lax.axis_index("block")
    owners = lax.dynamic_index_in_dim(owner_table, row, 0, keepdims=False)
    place, block_of, held = tables(owners)
    active = lax.dynamic_slice_in_dim(held, me * MOST, MOST, 0)
    count = owners.shape[0]
    blocks = gather_blocks(grad_partial, block_of, n_dp, 128)
    new_left, new_right, ready = precondition(active, blocks, left_factor, right_factor, 256)
    update = return_blocks(ready, place, count)
    return update[None], new_left, new_right


def solution(mesh):
    return jax.shard_map(
        functools.partial(local, mesh.shape["dp"]),
        mesh=mesh,
        in_specs=(
            P("dp", None, None, "block", None),
            P(),
            P("dp", "block", None, None, None),
            P("dp", "block", None, None, None),
        ),
        out_specs=(
            P("dp", None, "block", None),
            P("dp", "block", None, None, None),
            P("dp", "block", None, None, None),
        ),
        check_vma=False,
    )
```

time: 310 us -> 79.6 us (0.26); the launches traced: 306 us -> 79.4 us
  matrix products: 137 us -> 0 us
  Pallas kernels: 0 us -> 73.3 us
  waiting for transfers between devices: 56.7 us -> 0 us
  other arithmetic: 36.3 us -> 1.66 us
  blocking collectives: 33.2 us -> 0 us
  between operations: 26.6 us -> 0.67 us
  starting transfers between devices: 9.21 us -> 0 us
    dot_general x76 -> x0, matrix products: 137 us -> none  [the longest x32 41.2 us: inverse_root(): product = jnp.dot(shifted, vector, precision=lax.Precision.HIGHEST)]
    pallas_call x0 -> x3, Pallas kernels: none -> 73.3 us  [the longest x1 35.4 us: gather_blocks(): pl.pallas_call(functools.partial(gather_kernel, n_dp, count, lanes), name...]
    all_to_all x2 -> x0, waiting for transfers between devices: 56.7 us -> none  [the longest x1 48.4 us: sent_and_summed(): lax.all_to_all(parts, axis, split_axis=0, concat_axis=0, tiled=True)]
    all_to_all x2 -> x0, blocking collectives: 33.2 us -> none  [the longest x1 27.1 us: local(): lax.all_to_all(outgoing, BLOCK, split_axis=0, concat_axis=2, tiled=True)]
    reduce_sum x35 -> x2, other arithmetic: 23.5 us -> 0.18 us  [the longest x1 0.09 us: tables(): jnp.sum(same & (order[:, None] < order[None, :]), axis=0, dtype=jnp.int32)]
    all_to_all x2 -> x0, starting transfers between devices: 9.21 us -> none  [the longest x1 4.87 us: sent_and_summed(): lax.all_to_all(parts, axis, split_axis=0, concat_axis=0, tiled=True)]
    another operation x1 -> x0, other arithmetic: 4.8 us -> none  [local(): jnp.stack(new_rights)[None, None]]
    convert_element_type x2 -> x1, other arithmetic: 3.48 us -> 0.01 us  [tables(): return (place, block_of, jnp.any(holds, axis=1).astype(jnp.int32))]
  transfers between devices with their start and end apart: 2 -> 0, of which waited for: 2 -> 0; matrix products, arithmetic and copies ran while one was open for 3% -> 0% of each run, Pallas kernels for 0% -> 0%
where the time goes in v1:
time: 79.6 us; the launch traced here: 79.4 us
  Pallas kernels  73.3 us (92%)
  local copies, waits for them, and re-layouts  3.75 us (5%)
  other arithmetic  1.66 us (2%)
    pallas_call x1, Pallas kernels, gather_blocks(): pl.pallas_call(functools.partial(gather_kernel, n_dp, count, lanes), name...  35.4 us
    pallas_call x1, Pallas kernels, return_blocks(): pl.pallas_call(functools.partial(return_kernel, count), name='return_bloc...  19.8 us
    pallas_call x1, Pallas kernels, precondition(): pl.pallas_call(functools.partial(block_kernel, tall), name='precondition'...  18.1 us
    unnamed x5, local copies, waits for them, and re-layouts  2.99 us

profile of v1, /device:TPU:1, one launch (start us, length us, event | category | flops | bytes accessed | tf_op | source)
XLA Modules:
  0.0 79.4 jit_solution(4677146554545785504)
XLA Ops:
  0.6 0.7 fusion.3
  1.3 0.1 convert_reduce_fusion
  1.4 0.7 fusion.2
  2.1 0.7 multiply_add_fusion.place
  2.8 0.1 select_reduce_fusion.table
  2.9 0.1 fusion
  3.0 0.1 dynamic_slice.8.active
  3.1 0.0 copy-start
  3.1 2.2 %copy-done = f32[1,4,32,16,512]{4,3,2,1,0:T(8,128)S(1)} copy-done((f32[1,4,32,16,512]{4,3,2,1,0:T(8,128)S(1)}, f32[1,4,32,16,512]{4,3,2,1,0:T(8,128)}, u32[]{:S(2)}) %copy-start) | copy-done | bytes 4194328
  5.2 0.0 copy-start.1
  5.3 35.4 %gather_blocks.1.blocks = bf16[2,512,512]{2,1,0:T(8,128)(2,1)S(1)} custom-call(s32[64]{0:T(128)S(1)} %select_reduce_fusion.table, f32[1,4,32,16,512]{4,3,2,1,0:T(8,128)S(1)} %copy-done), custom_call_target="tpu_custom_call" | custom-call | tf_op jit(solution)/shard_map/gather_blocks/pallas_call | solution.py:158
  40.7 0.0 copy-done.1
  40.7 18.1 %precondition.1 = (f32[1,1,2,512,512]{4,3,2,1,0:T(8,128)}, f32[1,1,2,512,512]{4,3,2,1,0:T(8,128)}, bf16[2,512,512]{2,1,0:T(8,128)(2,1)S(1)}) custom-call(s32[2]{0:T(128)S(1)} %dynamic_slice.8.active, bf16[2,512,512]{2,1,0:T(8,128)(2,1)S(1)} %gather_blocks.1.blocks, f32[1,1,2,512,512]{4,3,2,1,0:T(8,128)S(1)} %copy-done.1, f32[1,1,2,512,512]{4,3,2,1,0:T(8,128)} %right.1), custom_call_target="tpu_custom_call" | custom-call | tf_op jit(solution)/shard_map/precondition/pallas_call | solution.py:319
  58.8 19.8 %return_blocks.1 = bf16[32,16,512]{2,1,0:T(8,128)(2,1)S(1)} custom-call(s32[32]{0:T(128)S(1)} %multiply_add_fusion.place, bf16[2,512,512]{2,1,0:T(8,128)(2,1)S(1)} %get-tuple-element.6.ready), custom_call_target="tpu_custom_call" | custom-call | tf_op jit(solution)/shard_map/return_blocks/pallas_call | solution.py:382
  78.6 0.8 %copy.8 = bf16[1,32,16,512]{3,2,1,0:T(8,128)(2,1)} copy(bf16[1,32,16,512]{3,2,1,0:T(8,128)(2,1)S(1)} %bitcast.11) | data formatting | bytes 1048576
  (1 shorter events, 0.0 us)
Async XLA Ops:
  3.1 2.2 %copy-start = (f32[1,4,32,16,512]{4,3,2,1,0:T(8,128)S(1)}, f32[1,4,32,16,512]{4,3,2,1,0:T(8,128)}, u32[]{:S(2)}) copy-start(f32[1,4,32,16,512]{4,3,2,1,0:T(8,128)} %grads.1) | copy-start | bytes 12582916
  5.2 35.4 %copy-start.1 = (f32[1,1,2,512,512]{4,3,2,1,0:T(8,128)S(1)}, f32[1,1,2,512,512]{4,3,2,1,0:T(8,128)}, u32[]{:S(2)}) copy-start(f32[1,1,2,512,512]{4,3,2,1,0:T(8,128)} %left.1) | copy-start | bytes 6291460

commit v2 on v0

v2 whole, which is shorter than its diff:
```python
import functools

import jax
import jax.numpy as jnp
from jax import lax
from jax.experimental import pallas as pl
from jax.experimental.pallas import tpu as pltpu
from jax.sharding import PartitionSpec as P

MOST = 2
POWER = 8
SPREAD = 13
MESH = pl.DeviceIdType.MESH
F32 = jnp.float32
BF16 = jnp.bfloat16
MIB = 1 << 20

decay_rate = 0.9
damping = 0.1
epsilon = 1e-06

A1, A2, A3, A4, A5 = 625 / 256, -500 / 256, 150 / 256, -20 / 256, 1 / 256
R0 = 25 / 16
R1 = (-5 - 3125 / 256) / 16
R2 = 3125 / 256 / 16
R3 = -1250 / 256 / 16
R4 = 250 / 256 / 16
R5 = -25 / 256 / 16
R6 = 1 / 256 / 16


def dot(a, b):
    return jnp.dot(a, b, preferred_element_type=F32)


def tiles_of(size, tall, broad):
    return [(i, j, pl.ds(i, tall), pl.ds(j, broad)) for j in range(0, size, broad) for i in range(0, size, tall)]


def plus_diagonal(value, i, j, amount):
    tall, broad = value.shape
    if i + tall <= j or j + broad <= i:
        return value
    down = lax.broadcasted_iota(jnp.int32, (tall, broad), 0) + i
    across = lax.broadcasted_iota(jnp.int32, (tall, broad), 1) + j
    return value + jnp.where(down == across, amount, F32(0))


def whole_sum(value):
    return jnp.sum(jnp.sum(value, axis=0, keepdims=True), axis=1, keepdims=True)


def largest_diagonal(factor, k, size):
    best = None
    for i in range(0, size, 128):
        part = factor[k, pl.ds(i, 128), pl.ds(i, 128)]
        down = lax.broadcasted_iota(jnp.int32, (128, 128), 0)
        across = lax.broadcasted_iota(jnp.int32, (128, 128), 1)
        part = jnp.where(down == across, part, F32(0))
        best = part if best is None else jnp.maximum(best, part)
    return jnp.max(jnp.max(best, axis=0, keepdims=True), axis=1, keepdims=True)


def precondition(slot, active, shape, blocks, flipped, factor, fresh, b, u, v, w, m, wide, result):
    size = blocks.shape[-1]
    tiles = tiles_of(size, *shape)
    chains = (2 * slot, 2 * slot + 1)

    def each(step):
        for k in chains:
            for i, j, rows, columns in tiles:
                step(k, i, j, rows, columns)

    flipped[slot] = blocks[slot].T
    original = blocks[slot].astype(F32)
    energy_in = whole_sum(original * original)
    tops = {k: decay_rate * largest_diagonal(factor, k, size) + ((1.0 - decay_rate) / size) * energy_in + damping for k in chains}
    shrink = {k: 1.0 / tops[k] for k in chains}
    columns_sum = {k: {} for k in chains}
    keep = jnp.where(active, F32(decay_rate), F32(1.0))
    add = jnp.where(active, F32((1.0 - decay_rate) / size), F32(0.0))

    def gram(k, i, j, rows, columns):
        first, second = (blocks, flipped) if k % 2 == 0 else (flipped, blocks)
        old = factor[k, rows, columns]
        product = dot(first[slot, rows, :], second[slot, :, columns])
        new = keep * old + add * product
        fresh[k % 2][slot, rows, columns] = new
        value = plus_diagonal(new * shrink[k], i, j, damping * shrink[k])
        b[k, rows, columns] = value.astype(BF16)
        part = jnp.sum(value, axis=0, keepdims=True)
        columns_sum[k][j] = columns_sum[k][j] + part if j in columns_sum[k] else part

    def square(k, i, j, rows, columns):
        u[k, rows, columns] = dot(b[k, rows, :], b[k, :, columns]).astype(BF16)

    def cube(k, i, j, rows, columns):
        w[k, rows, columns] = dot(b[k, rows, :], u[k, :, columns]).astype(BF16)

    each(gram)
    each(square)
    each(cube)

    vector = {
        k: jnp.concatenate([columns_sum[k][j] for j in sorted(columns_sum[k])], axis=1) for k in chains
    }
    length = {}
    for turn, matrix in enumerate((w, w, b)):
        for k in chains:
            vector[k] = vector[k] * lax.rsqrt(jnp.sum(vector[k] * vector[k], axis=1, keepdims=True))
        for k in chains:
            high = vector[k].astype(BF16)
            low = (vector[k] - high.astype(F32)).astype(BF16)
            both = dot(jnp.concatenate([high, low], axis=0), matrix[k])
            vector[k] = both[0:1] + both[1:2]
    for k in chains:
        length[k] = jnp.sqrt(jnp.sum(vector[k] * vector[k], axis=1, keepdims=True))
    c1 = {k: 1.0 / (1.25 * length[k]) for k in chains}
    c2 = {k: c1[k] * c1[k] for k in chains}
    c3 = {k: c2[k] * c1[k] for k in chains}
    scale = {k: lax.rsqrt(jnp.sqrt((1.25 * length[k]) * tops[k])) for k in chains}

    def thin(scalar):
        return scalar.astype(BF16)

    def mixed(k, i, j, rows, columns):
        v[k, rows, columns] = (
            thin(A4 * c1[k]) * b[k, rows, columns] + thin(A5 * c2[k]) * u[k, rows, columns]
        )

    def second(k, i, j, rows, columns):
        value = c3[k] * dot(w[k, rows, :], v[k, :, columns])
        small = thin(A2 * c2[k]) * u[k, rows, columns] + thin(A3 * c3[k]) * w[k, rows, columns]
        value += (A1 * c1[k]) * b[k, rows, columns].astype(F32) + small.astype(F32)
        m[k, rows, columns] = value.astype(BF16)

    def square_again(k, i, j, rows, columns):
        u[k, rows, columns] = dot(m[k, rows, :], m[k, :, columns]).astype(BF16)

    def cube_again(k, i, j, rows, columns):
        product = dot(m[k, rows, :], u[k, :, columns]).astype(BF16)
        w[k, rows, columns] = product
        v[k, rows, columns] = (
            BF16(R4) * m[k, rows, columns] + BF16(R5) * u[k, rows, columns] + BF16(R6) * product
        )

    def tail(k, i, j, rows, columns):
        small = BF16(R2) * u[k, rows, columns] + BF16(R3) * w[k, rows, columns]
        value = dot(w[k, rows, :], v[k, :, columns]) + small.astype(F32)
        m[k, rows, columns] = (value + R1 * m[k, rows, columns].astype(F32)).astype(BF16)

    def root(k, i, j, rows, columns):
        value = (1.25 * scale[k]) * m[k, rows, columns].astype(F32)
        value -= (0.25 * R0 * scale[k] * c1[k]) * b[k, rows, columns].astype(F32)
        value -= (0.25 * scale[k] * c1[k]) * dot(b[k, rows, :], m[k, :, columns])
        v[k, rows, columns] = plus_diagonal(value, i, j, (1.25 * R0) * scale[k]).astype(BF16)

    for step in (mixed, second, square_again, cube_again, tail, root):
        each(step)

    one, two = chains
    for i, j, rows, columns in tiles:
        u[one, rows, columns] = dot(v[one, rows, :], blocks[slot, :, columns]).astype(BF16)
    energy = jnp.zeros((1, 1), F32)
    for i, j, rows, columns in tiles:
        shaped = dot(u[one, rows, :], v[two, :, columns])
        wide[rows, columns] = shaped
        energy += whole_sum(shaped * shaped)
    graft = jnp.sqrt(energy_in / (size * size)) / jnp.sqrt(energy / (size * size) + epsilon)
    for i, j, rows, columns in tiles:
        result[slot, rows, columns] = (wide[rows, columns] * graft).astype(BF16)


def step_kernel(
    n_dp, count, lanes, shape, owner_table, grads, left, right, update, left_new, right_new, owners_v, owners_s,
    place_v, place_s, block_v, block_s, stage, raw, raw_in, cross, cross_in, both, both_in, summed, outgoing,
    blocks, flipped, factor, b, u, v, w, m, wide, ready, back, load_sem, factor_sem, table_sem, x_send, x_recv,
    o_send, o_recv, r_send, r_recv,
):
    row, me = lax.axis_index("dp"), lax.axis_index("block")
    stripe = grads.shape[3]
    half = count // 2
    chunks = grads.shape[4] // lanes
    near, behind, far = lax.rem(row + 1, n_dp), lax.rem(row + n_dp - 1, n_dp), lax.rem(row + 2, n_dp)

    table_loads = [
        pltpu.make_async_copy(owner_table, owners_v, table_sem.at[0]),
        pltpu.make_async_copy(owner_table, owners_s, table_sem.at[1]),
    ]
    loads = [
        pltpu.make_async_copy(grads.at[0, d], stage.at[n], load_sem.at[n])
        for n, d in enumerate((far, near, behind, row))
    ]
    factor_loads = [
        pltpu.make_async_copy((left, right)[k % 2].at[0, 0, k // 2], factor.at[k], factor_sem.at[k])
        for k in range(2 * MOST)
    ]
    for load in (*loads, *table_loads):
        load.start()

    def partner(k):
        return lax.rem(me + SPREAD * k, count)

    barrier = pltpu.get_barrier_semaphore()
    for peer in (near, behind):
        pl.semaphore_signal(barrier, inc=1, device_id=(peer, me), device_id_type=MESH)

    def greet(k, carry):
        pl.semaphore_signal(barrier, inc=1, device_id=(row, partner(k)), device_id_type=MESH)
        return carry

    lax.fori_loop(1, count, greet, 0)

    own_rows = pl.ds(pl.multiple_of(me * stripe, stripe), stripe)
    halves = (pl.ds(0, half), pl.ds(half, half))
    towards = (near, behind)

    def cut(n, part, c):
        return stage[n, halves[part], :, pl.ds(c * lanes, lanes)]

    def x_copy(kind, way, c, src, dst):
        return pltpu.make_async_remote_copy(
            src_ref=src.at[way, c],
            dst_ref=dst.at[way, c],
            send_sem=x_send.at[kind, way, c],
            recv_sem=x_recv.at[kind, way, c],
            device_id=(towards[way], me),
            device_id_type=MESH,
        )

    raws = [[x_copy(0, way, c, raw, raw_in) for way in range(2)] for c in range(chunks)]
    crosses = [[x_copy(1, way, c, cross, cross_in) for way in range(2)] for c in range(chunks)]
    boths = [[x_copy(2, way, c, both, both_in) for way in range(2)] for c in range(chunks)]

    def dispatch(c):
        columns = pl.ds(c * lanes, lanes)
        for way in range(2):
            crosses[c][way].wait_recv()
            boths[c][way].wait_recv()
        for part in range(2):
            total = cut(3, part, c) + both_in[part, c].astype(F32) + cross_in[1 - part, c].astype(F32)
            summed[c, halves[part]] = total.astype(BF16)

        def send(k, carry):
            o = partner(k)
            for s in range(MOST):
                outgoing[c, o, s] = summed[c, block_s[0, o * MOST + s]]
            pltpu.make_async_remote_copy(
                src_ref=outgoing.at[c, o],
                dst_ref=blocks.at[:, own_rows, columns],
                send_sem=o_send.at[c],
                recv_sem=o_recv.at[c],
                device_id=(row, o),
                device_id_type=MESH,
            ).start()
            return carry

        lax.fori_loop(1, count, send, 0)
        for s in range(MOST):
            blocks[s, own_rows, columns] = summed[c, block_s[0, me * MOST + s]]

    loads[0].wait()
    for c in range(chunks):
        for way in range(2):
            raw[way, c] = cut(0, way, c).astype(BF16)
    loads[1].wait()
    loads[2].wait()
    for c in range(chunks):
        for way in range(2):
            cross[way, c] = cut(1 + way, 1 - way, c).astype(BF16)
    pl.semaphore_wait(barrier, count + 1)
    for way in range(2):
        raws[0][way].start()
    for way in range(2):
        crosses[0][way].start()
    for c in range(1, chunks):
        for way in range(2):
            raws[c][way].start()

    for load in table_loads:
        load.wait()
    owners = owners_v[pl.ds(row, 1), :]
    order = lax.broadcasted_iota(jnp.int32, owners.shape, 1)

    def count_same(j, ranks):
        same = (owners == owners_s[row, j]) & (order > j)
        return ranks + jnp.where(same, 1, 0)

    places = owners * MOST + lax.fori_loop(0, count, count_same, jnp.zeros_like(owners))
    place_v[...] = places
    place_copy = pltpu.make_async_copy(place_v, place_s, table_sem.at[2])
    place_copy.start()
    place_copy.wait()
    slots = lax.broadcasted_iota(jnp.int32, block_v.shape, 1)

    def fill(j, held):
        return jnp.where(slots == place_s[0, j], j, held)

    block_v[...] = lax.fori_loop(0, count, fill, jnp.zeros_like(slots))
    block_copy = pltpu.make_async_copy(block_v, block_s, table_sem.at[3])
    block_copy.start()
    block_copy.wait()
    loads[3].wait()
    for load in factor_loads:
        load.start()

    for c in range(chunks):
        if c > 0:
            for way in range(2):
                crosses[c][way].start()
        for way in range(2):
            raws[c][way].wait_recv()
            both[way, c] = (cut(1 + way, way, c) + raw_in[way, c].astype(F32)).astype(BF16)
            boths[c][way].start()
        if c > 0:
            dispatch(c - 1)
    dispatch(chunks - 1)
    for load in factor_loads:
        load.wait()
    for c in range(chunks):
        arrived = outgoing.at[c, pl.ds(0, count - 1)]
        pltpu.make_async_copy(arrived, arrived, o_recv.at[c]).wait()

    for slot in range(MOST):
        used = jnp.where(places == me * MOST + slot, F32(1), F32(0))
        active = jnp.max(used, axis=1, keepdims=True) > 0.5
        precondition(
            slot, active, shape, blocks, flipped, factor, (left_new, right_new), b, u, v, w, m, wide, ready
        )

        def give(k, carry):
            o = partner(k)
            pltpu.make_async_remote_copy(
                src_ref=ready.at[slot, pl.ds(pl.multiple_of(o * stripe, stripe), stripe)],
                dst_ref=back.at[me * MOST + slot],
                send_sem=r_send.at[slot],
                recv_sem=r_recv.at[slot],
                device_id=(row, o),
                device_id_type=MESH,
            ).start()
            return carry

        lax.fori_loop(1, count, give, 0)
        back[me * MOST + slot] = ready[slot, own_rows]

    for c in range(chunks):
        for way in range(2):
            raws[c][way].wait_send()
            crosses[c][way].wait_send()
            boths[c][way].wait_send()
        arrived = outgoing.at[c, pl.ds(0, count - 1)]
        pltpu.make_async_copy(arrived, arrived, o_send.at[c]).wait()
    for slot in range(MOST):
        arrived = back.at[pl.ds(0, count - 1)]
        pltpu.make_async_copy(arrived, arrived, r_recv.at[slot]).wait()
        pltpu.make_async_copy(arrived, arrived, r_send.at[slot]).wait()

    def put(j, carry):
        update[j] = back[place_s[0, j]]
        return carry

    lax.fori_loop(0, count, put, 0)


def whole_step(owner_table, grads, left, right, n_dp, lanes, shape):
    _, _, count, stripe, size = grads.shape
    chunks = size // lanes
    part = pltpu.VMEM((2, chunks, count // 2, stripe, lanes), BF16)
    thin = pltpu.VMEM((2 * MOST, size, size), BF16)
    pair = pltpu.VMEM((MOST, size, size), BF16)
    slots = -(-MOST * count // 128) * 128
    DMA = pltpu.SemaphoreType.DMA
    hbm, vmem = pl.BlockSpec(memory_space=pltpu.HBM), pl.BlockSpec(memory_space=pltpu.VMEM)
    return pl.pallas_call(
        functools.partial(step_kernel, n_dp, count, lanes, shape),
        name="shampoo_step",
        out_shape=(
            jax.ShapeDtypeStruct((count, stripe, size), BF16),
            jax.ShapeDtypeStruct((MOST, size, size), F32),
            jax.ShapeDtypeStruct((MOST, size, size), F32),
        ),
        in_specs=[hbm, hbm, hbm, hbm],
        out_specs=(vmem, vmem, vmem),
        scratch_shapes=[
            pltpu.VMEM((n_dp, count), jnp.int32),
            pltpu.SMEM((n_dp, count), jnp.int32),
            pltpu.VMEM((1, count), jnp.int32),
            pltpu.SMEM((1, count), jnp.int32),
            pltpu.VMEM((1, slots), jnp.int32),
            pltpu.SMEM((1, slots), jnp.int32),
            pltpu.VMEM((4, count, stripe, size), F32),
            part, part, part, part, part, part,
            pltpu.VMEM((chunks, count, stripe, lanes), BF16),
            pltpu.VMEM((chunks, count, MOST, stripe, lanes), BF16),
            pair, pair,
            pltpu.VMEM((2 * MOST, size, size), F32),
            thin, thin, thin, thin, thin,
            pltpu.VMEM((size, size), F32),
            pair,
            pltpu.VMEM((MOST * count, stripe, size), BF16),
            DMA((4,)), DMA((2 * MOST,)), DMA((4,)), DMA((3, 2, chunks)), DMA((3, 2, chunks)),
            DMA((chunks,)), DMA((chunks,)), DMA((MOST,)), DMA((MOST,)),
        ],
        compiler_params=pltpu.CompilerParams(
            collective_id=0, has_side_effects=True, vmem_limit_bytes=48 * MIB
        ),
    )(owner_table, grads, left, right)


def store_kernel(*refs):
    sources, targets, sems = refs[:3], refs[3:6], refs[6]
    copies = [pltpu.make_async_copy(s, t, sems.at[n]) for n, (s, t) in enumerate(zip(sources, targets))]
    for copy in copies:
        copy.start()
    for copy in copies:
        copy.wait()


def store(*values):
    return pl.pallas_call(
        store_kernel,
        name="store",
        out_shape=tuple(jax.ShapeDtypeStruct(x.shape, x.dtype) for x in values),
        in_specs=[pl.BlockSpec(memory_space=pltpu.VMEM)] * 3,
        out_specs=tuple([pl.BlockSpec(memory_space=pltpu.HBM)] * 3),
        scratch_shapes=[pltpu.SemaphoreType.DMA((3,))],
        compiler_params=pltpu.CompilerParams(vmem_limit_bytes=8 * MIB),
    )(*values)


def local(n_dp, grad_partial, owner_table, left_factor, right_factor):
    values = whole_step(owner_table, grad_partial, left_factor, right_factor, n_dp, 128, (512, 256))
    update, new_left, new_right = store(*values)
    return update[None], new_left[None, None], new_right[None, None]


def solution(mesh):
    return jax.shard_map(
        functools.partial(local, mesh.shape["dp"]),
        mesh=mesh,
        in_specs=(
            P("dp", None, None, "block", None),
            P(),
            P("dp", "block", None, None, None),
            P("dp", "block", None, None, None),
        ),
        out_specs=(
            P("dp", None, "block", None),
            P("dp", "block", None, None, None),
            P("dp", "block", None, None, None),
        ),
        check_vma=False,
    )
```

time: 310 us -> 62.5 us (0.20); the launches traced: 306 us -> 62.3 us
  matrix products: 137 us -> 0 us
  Pallas kernels: 0 us -> 60.9 us
  waiting for transfers between devices: 56.7 us -> 0 us
  other arithmetic: 36.3 us -> 0 us
  blocking collectives: 33.2 us -> 0 us
  between operations: 26.6 us -> 0.81 us
  starting transfers between devices: 9.21 us -> 0 us
  local copies, waits for them, and re-layouts: 6.66 us -> 0.67 us
    dot_general x76 -> x0, matrix products: 137 us -> none  [the longest x32 41.2 us: inverse_root(): product = jnp.dot(shifted, vector, precision=lax.Precision.HIGHEST)]
    pallas_call x0 -> x2, Pallas kernels: none -> 60.9 us  [the longest x1 58.6 us: whole_step(): pl.pallas_call(functools.partial(step_kernel, n_dp, count, lanes, shape),...]
    all_to_all x2 -> x0, waiting for transfers between devices: 56.7 us -> none  [the longest x1 48.4 us: sent_and_summed(): lax.all_to_all(parts, axis, split_axis=0, concat_axis=0, tiled=True)]
    all_to_all x2 -> x0, blocking collectives: 33.2 us -> none  [the longest x1 27.1 us: local(): lax.all_to_all(outgoing, BLOCK, split_axis=0, concat_axis=2, tiled=True)]
    reduce_sum x35 -> x0, other arithmetic: 23.5 us -> none  [the longest x32 19.8 us: inverse_root(): length = jnp.sqrt(jnp.sum(product * product))]
    all_to_all x2 -> x0, starting transfers between devices: 9.21 us -> none  [the longest x1 4.87 us: sent_and_summed(): lax.all_to_all(parts, axis, split_axis=0, concat_axis=0, tiled=True)]
    another operation x1 -> x0, other arithmetic: 4.8 us -> none  [local(): jnp.stack(new_rights)[None, None]]
    convert_element_type x2 -> x0, other arithmetic: 3.48 us -> none  [precondition(): return ((shaped * graft_scale).astype(jnp.bfloat16), new_left, new_right)]
  transfers between devices with their start and end apart: 2 -> 0, of which waited for: 2 -> 0; matrix products, arithmetic and copies ran while one was open for 3% -> 0% of each run, Pallas kernels for 0% -> 0%
where the time goes in v2:
time: 62.5 us; the launch traced here: 62.3 us
  Pallas kernels  60.9 us (97%)
  between operations  0.81 us (1%)
  local copies, waits for them, and re-layouts  0.67 us (1%)
    pallas_call x1, Pallas kernels, whole_step(): pl.pallas_call(functools.partial(step_kernel, n_dp, count, lanes, shape),...  58.6 us
    pallas_call x1, Pallas kernels, store(): pl.pallas_call(store_kernel, name='store', out_shape=tuple((jax.ShapeDtyp...  2.21 us

profile of v2, /device:TPU:1, one launch (start us, length us, event | category | flops | bytes accessed | tf_op | source)
XLA Modules:
  0.0 62.3 jit_solution(2520022017604175275)
XLA Ops:
  0.6 0.0 copy-start
  0.6 0.7 %copy-done = s32[4,32]{1,0:T(4,128)S(1)} copy-done((s32[4,32]{1,0:T(4,128)S(1)}, s32[4,32]{1,0:T(4,128)}, u32[]{:S(2)}) %copy-start) | copy-done | bytes 536
  1.3 58.6 %shampoo_step.1 = (bf16[32,16,512]{2,1,0:T(8,128)(2,1)S(1)}, f32[2,512,512]{2,1,0:T(8,128)S(1)}, f32[2,512,512]{2,1,0:T(8,128)S(1)}) custom-call(s32[4,32]{1,0:T(4,128)S(1)} %copy-done, f32[1,4,32,16,512]{4,3,2,1,0:T(8,128)} %grads.1, f32[1,1,2,512,512]{4,3,2,1,0:T(8,128)} %left.1, f32[1,1,2,512,512]{4,3,2,1,0:T(8,128)} %right.1), custom_call_target="tpu_custom_call" | custom-call | tf_op jit(solution)/shard_map/shampoo_step/pallas_call | solution.py:374
  60.0 2.2 %store.1 = (bf16[32,16,512]{2,1,0:T(8,128)(2,1)}, f32[2,512,512]{2,1,0:T(8,128)}, f32[2,512,512]{2,1,0:T(8,128)}) custom-call(bf16[32,16,512]{2,1,0:T(8,128)(2,1)S(1)} %get-tuple-element.9.refs_0_, f32[2,512,512]{2,1,0:T(8,128)S(1)} %get-tuple-element.10.refs_1_, f32[2,512,512]{2,1,0:T(8,128)S(1)} %get-tuple-element.11.refs_2_), custom_call_target="tpu_custom_call" | custom-call | tf_op jit(solution)/shard_map/store/pallas_call | solution.py:420
Async XLA Ops:
  0.6 0.7 %copy-start = (s32[4,32]{1,0:T(4,128)S(1)}, s32[4,32]{1,0:T(4,128)}, u32[]{:S(2)}) copy-start(s32[4,32]{1,0:T(4,128)} %owner_table.1) | copy-start | bytes 1540

commit v3 on v2

--- a/solution.py
+++ b/solution.py
@@ -9,11 +9,22 @@
 
 MOST = 2
 POWER = 8
-SPREAD = 13
+SIDE = 4
+
+
+def distance(hop):
+    return sum(min(steps, SIDE - steps) for steps in hop[:2])
+
+
+HOPS = sorted(
+    ((z, y, core) for z in range(SIDE) for y in range(SIDE) for core in range(2) if (z, y, core) != (0, 0, 0)),
+    key=lambda hop: (-distance(hop), (hop[0] + hop[1]) % 2, hop),
+)
 MESH = pl.DeviceIdType.MESH
 F32 = jnp.float32
 BF16 = jnp.bfloat16
 MIB = 1 << 20
+PIECES = 4
 
 decay_rate = 0.9
 damping = 0.1
@@ -31,10 +42,6 @@
 
 def dot(a, b):
     return jnp.dot(a, b, preferred_element_type=F32)
-
-
-def tiles_of(size, tall, broad):
-    return [(i, j, pl.ds(i, tall), pl.ds(j, broad)) for j in range(0, size, broad) for i in range(0, size, tall)]
 
 
 def plus_diagonal(value, i, j, amount):
@@ -61,51 +68,78 @@
     return jnp.max(jnp.max(best, axis=0, keepdims=True), axis=1, keepdims=True)
 
 
-def precondition(slot, active, shape, blocks, flipped, factor, fresh, b, u, v, w, m, wide, result):
+def absorb(slot, c, lanes, blocks, flipped, sums, last):
+    columns = pl.ds(c * lanes, lanes)
+    piece = blocks[slot, :, columns]
+    flipped[slot, columns, :] = piece.T
+    wide = piece.astype(F32)
+    energy = jnp.sum(wide * wide, axis=0, keepdims=True)
+    one, two = 2 * slot, 2 * slot + 1
+    if not last:
+        product = dot(piece, flipped[slot, columns, :])
+        sums[one] = product if c == 0 else sums[one] + product
+    seen = (c + 1) * lanes
+    product = dot(flipped[slot, pl.ds(0, seen), :], piece)
+    sums[two, pl.ds(0, seen), columns] = product
+    if c > 0:
+        sums[two, columns, pl.ds(0, c * lanes)] = product[: c * lanes].T
+    return energy
+
+
+def precondition(slot, active, tile, lanes, energy_in, tops, blocks, flipped, sums, factor, fresh, b, u, v, w, m, wide, result):
     size = blocks.shape[-1]
-    tiles = tiles_of(size, *shape)
     chains = (2 * slot, 2 * slot + 1)
-
-    def each(step):
-        for k in chains:
-            for i, j, rows, columns in tiles:
-                step(k, i, j, rows, columns)
-
-    flipped[slot] = blocks[slot].T
-    original = blocks[slot].astype(F32)
-    energy_in = whole_sum(original * original)
-    tops = {k: decay_rate * largest_diagonal(factor, k, size) + ((1.0 - decay_rate) / size) * energy_in + damping for k in chains}
+    offsets = range(0, size, tile)
+    energy_in = jnp.sum(energy_in, axis=1, keepdims=True)
+    grown = ((1.0 - decay_rate) / size) * energy_in + damping
+    tops = {k: tops[k] + grown for k in chains}
     shrink = {k: 1.0 / tops[k] for k in chains}
     columns_sum = {k: {} for k in chains}
     keep = jnp.where(active, F32(decay_rate), F32(1.0))
     add = jnp.where(active, F32((1.0 - decay_rate) / size), F32(0.0))
 
     def gram(k, i, j, rows, columns):
-        first, second = (blocks, flipped) if k % 2 == 0 else (flipped, blocks)
-        old = factor[k, rows, columns]
-        product = dot(first[slot, rows, :], second[slot, :, columns])
-        new = keep * old + add * product
+        product = sums[k, rows, columns]
+        if k % 2 == 0:
+            final = pl.ds(size - lanes, lanes)
+            product += dot(blocks[slot, rows, final], flipped[slot, final, columns])
+        new = keep * factor[k, rows, columns] + add * product
         fresh[k % 2][slot, rows, columns] = new
         value = plus_diagonal(new * shrink[k], i, j, damping * shrink[k])
         b[k, rows, columns] = value.astype(BF16)
         part = jnp.sum(value, axis=0, keepdims=True)
         columns_sum[k][j] = columns_sum[k][j] + part if j in columns_sum[k] else part
 
+    for k in chains:
+        for j in offsets:
+            for i in offsets:
+                gram(k, i, j, pl.ds(i, tile), pl.ds(j, tile))
+
+    def each(step, *targets):
+        for k in chains:
+            for j in offsets:
+                for i in range(0, j + 1, tile):
+                    rows, columns = pl.ds(i, tile), pl.ds(j, tile)
+                    values = step(k, i, j, rows, columns)
+                    for target, value in zip(targets, values):
+                        target[k, rows, columns] = value
+                        if i != j:
+                            target[k, columns, rows] = value.T
+
     def square(k, i, j, rows, columns):
-        u[k, rows, columns] = dot(b[k, rows, :], b[k, :, columns]).astype(BF16)
+        return (dot(b[k, rows, :], b[k, :, columns]).astype(BF16),)
 
     def cube(k, i, j, rows, columns):
-        w[k, rows, columns] = dot(b[k, rows, :], u[k, :, columns]).astype(BF16)
-
-    each(gram)
-    each(square)
-    each(cube)
+        return (dot(b[k, rows, :], u[k, :, columns]).astype(BF16),)
+
+    each(square, u)
+    each(cube, w)
 
     vector = {
         k: jnp.concatenate([columns_sum[k][j] for j in sorted(columns_sum[k])], axis=1) for k in chains
     }
     length = {}
-    for turn, matrix in enumerate((w, w, b)):
+    for matrix in (w, w, b):
         for k in chains:
             vector[k] = vector[k] * lax.rsqrt(jnp.sum(vector[k] * vector[k], axis=1, keepdims=True))
         for k in chains:
@@ -123,64 +157,65 @@
     def thin(scalar):
         return scalar.astype(BF16)
 
-    def mixed(k, i, j, rows, columns):
-        v[k, rows, columns] = (
-            thin(A4 * c1[k]) * b[k, rows, columns] + thin(A5 * c2[k]) * u[k, rows, columns]
-        )
+    for k in chains:
+        v[k] = thin(A4 * c1[k]) * b[k] + thin(A5 * c2[k]) * u[k]
 
     def second(k, i, j, rows, columns):
         value = c3[k] * dot(w[k, rows, :], v[k, :, columns])
         small = thin(A2 * c2[k]) * u[k, rows, columns] + thin(A3 * c3[k]) * w[k, rows, columns]
         value += (A1 * c1[k]) * b[k, rows, columns].astype(F32) + small.astype(F32)
-        m[k, rows, columns] = value.astype(BF16)
+        return (value.astype(BF16),)
 
     def square_again(k, i, j, rows, columns):
-        u[k, rows, columns] = dot(m[k, rows, :], m[k, :, columns]).astype(BF16)
+        return (dot(m[k, rows, :], m[k, :, columns]).astype(BF16),)
 
     def cube_again(k, i, j, rows, columns):
         product = dot(m[k, rows, :], u[k, :, columns]).astype(BF16)
-        w[k, rows, columns] = product
-        v[k, rows, columns] = (
-            BF16(R4) * m[k, rows, columns] + BF16(R5) * u[k, rows, columns] + BF16(R6) * product
-        )
+        mixed = BF16(R4) * m[k, rows, columns] + BF16(R5) * u[k, rows, columns] + BF16(R6) * product
+        return (product, mixed)
 
     def tail(k, i, j, rows, columns):
         small = BF16(R2) * u[k, rows, columns] + BF16(R3) * w[k, rows, columns]
         value = dot(w[k, rows, :], v[k, :, columns]) + small.astype(F32)
-        m[k, rows, columns] = (value + R1 * m[k, rows, columns].astype(F32)).astype(BF16)
+        return ((value + R1 * m[k, rows, columns].astype(F32)).astype(BF16),)
 
     def root(k, i, j, rows, columns):
         value = (1.25 * scale[k]) * m[k, rows, columns].astype(F32)
         value -= (0.25 * R0 * scale[k] * c1[k]) * b[k, rows, columns].astype(F32)
         value -= (0.25 * scale[k] * c1[k]) * dot(b[k, rows, :], m[k, :, columns])
-        v[k, rows, columns] = plus_diagonal(value, i, j, (1.25 * R0) * scale[k]).astype(BF16)
-
-    for step in (mixed, second, square_again, cube_again, tail, root):
-        each(step)
+        return (plus_diagonal(value, i, j, (1.25 * R0) * scale[k]).astype(BF16),)
+
+    each(second, m)
+    each(square_again, u)
+    each(cube_again, w, v)
+    each(tail, m)
+    each(root, v)
 
     one, two = chains
-    for i, j, rows, columns in tiles:
-        u[one, rows, columns] = dot(v[one, rows, :], blocks[slot, :, columns]).astype(BF16)
+    for j in offsets:
+        columns = pl.ds(j, tile)
+        u[one, :, columns] = dot(v[one], blocks[slot, :, columns]).astype(BF16)
     energy = jnp.zeros((1, 1), F32)
-    for i, j, rows, columns in tiles:
-        shaped = dot(u[one, rows, :], v[two, :, columns])
-        wide[rows, columns] = shaped
+    for j in offsets:
+        columns = pl.ds(j, tile)
+        shaped = dot(u[one], v[two, :, columns])
+        wide[:, columns] = shaped
         energy += whole_sum(shaped * shaped)
     graft = jnp.sqrt(energy_in / (size * size)) / jnp.sqrt(energy / (size * size) + epsilon)
-    for i, j, rows, columns in tiles:
-        result[slot, rows, columns] = (wide[rows, columns] * graft).astype(BF16)
+    result[slot] = (wide[...] * graft).astype(BF16)
 
 
 def step_kernel(
-    n_dp, count, lanes, shape, owner_table, grads, left, right, update, left_new, right_new, owners_v, owners_s,
+    n_dp, count, lanes, tile, owner_table, grads, left, right, update, left_new, right_new, owners_v, owners_s,
     place_v, place_s, block_v, block_s, stage, raw, raw_in, cross, cross_in, both, both_in, summed, outgoing,
-    blocks, flipped, factor, b, u, v, w, m, wide, ready, back, load_sem, factor_sem, table_sem, x_send, x_recv,
+    blocks, flipped, sums, factor, b, u, v, w, m, wide, ready, back, load_sem, factor_sem, table_sem, x_send, x_recv,
     o_send, o_recv, r_send, r_recv,
 ):
     row, me = lax.axis_index("dp"), lax.axis_index("block")
     stripe = grads.shape[3]
     half = count // 2
-    chunks = grads.shape[4] // lanes
+    size = grads.shape[4]
+    chunks = size // lanes
     near, behind, far = lax.rem(row + 1, n_dp), lax.rem(row + n_dp - 1, n_dp), lax.rem(row + 2, n_dp)
 
     table_loads = [
@@ -198,18 +233,19 @@
     for load in (*loads, *table_loads):
         load.start()
 
-    def partner(k):
-        return lax.rem(me + SPREAD * k, count)
+    my_chip, my_core = (me // (2 * SIDE), lax.rem(me // 2, SIDE)), lax.rem(me, 2)
+
+    def partner(hop):
+        z, y, core = hop
+        chip = lax.rem(my_chip[0] + z, SIDE) * SIDE + lax.rem(my_chip[1] + y, SIDE)
+        return chip * 2 + lax.rem(my_core + core, 2)
 
     barrier = pltpu.get_barrier_semaphore()
     for peer in (near, behind):
         pl.semaphore_signal(barrier, inc=1, device_id=(peer, me), device_id_type=MESH)
 
-    def greet(k, carry):
-        pl.semaphore_signal(barrier, inc=1, device_id=(row, partner(k)), device_id_type=MESH)
-        return carry
-
-    lax.fori_loop(1, count, greet, 0)
+    for hop in HOPS:
+        pl.semaphore_signal(barrier, inc=1, device_id=(row, partner(hop)), device_id_type=MESH)
 
     own_rows = pl.ds(pl.multiple_of(me * stripe, stripe), stripe)
     halves = (pl.ds(0, half), pl.ds(half, half))
@@ -241,8 +277,8 @@
             total = cut(3, part, c) + both_in[part, c].astype(F32) + cross_in[1 - part, c].astype(F32)
             summed[c, halves[part]] = total.astype(BF16)
 
-        def send(k, carry):
-            o = partner(k)
+        for hop in HOPS:
+            o = partner(hop)
             for s in range(MOST):
                 outgoing[c, o, s] = summed[c, block_s[0, o * MOST + s]]
             pltpu.make_async_remote_copy(
@@ -253,29 +289,37 @@
                 device_id=(row, o),
                 device_id_type=MESH,
             ).start()
-            return carry
-
-        lax.fori_loop(1, count, send, 0)
         for s in range(MOST):
             blocks[s, own_rows, columns] = summed[c, block_s[0, me * MOST + s]]
 
-    loads[0].wait()
-    for c in range(chunks):
+    def start_raw(c):
         for way in range(2):
             raw[way, c] = cut(0, way, c).astype(BF16)
+        if c == 0:
+            pl.semaphore_wait(barrier, count + 1)
+        for way in range(2):
+            raws[c][way].start()
+
+    def start_cross(c):
+        for way in range(2):
+            cross[way, c] = cut(1 + way, 1 - way, c).astype(BF16)
+            crosses[c][way].start()
+
+    energies = [[] for _ in range(MOST)]
+
+    def arrive(c, slots_here):
+        if slots_here[0] == 0:
+            arrived = outgoing.at[c, pl.ds(0, count - 1)]
+            pltpu.make_async_copy(arrived, arrived, o_recv.at[c]).wait()
+        for slot in slots_here:
+            energies[slot].append(absorb(slot, c, lanes, blocks, flipped, sums, c == chunks - 1))
+
+    loads[0].wait()
+    start_raw(0)
     loads[1].wait()
     loads[2].wait()
-    for c in range(chunks):
-        for way in range(2):
-            cross[way, c] = cut(1 + way, 1 - way, c).astype(BF16)
-    pl.semaphore_wait(barrier, count + 1)
-    for way in range(2):
-        raws[0][way].start()
-    for way in range(2):
-        crosses[0][way].start()
-    for c in range(1, chunks):
-        for way in range(2):
-            raws[c][way].start()
+    start_cross(0)
+    start_raw(1)
 
     for load in table_loads:
         load.wait()
@@ -306,30 +350,35 @@
 
     for c in range(chunks):
         if c > 0:
-            for way in range(2):
-                crosses[c][way].start()
+            start_cross(c)
+            if c + 1 < chunks:
+                start_raw(c + 1)
         for way in range(2):
             raws[c][way].wait_recv()
             both[way, c] = (cut(1 + way, way, c) + raw_in[way, c].astype(F32)).astype(BF16)
             boths[c][way].start()
         if c > 0:
             dispatch(c - 1)
+        if c > 1:
+            arrive(c - 2, range(MOST))
     dispatch(chunks - 1)
     for load in factor_loads:
         load.wait()
-    for c in range(chunks):
-        arrived = outgoing.at[c, pl.ds(0, count - 1)]
-        pltpu.make_async_copy(arrived, arrived, o_recv.at[c]).wait()
+    tops = {k: decay_rate * largest_diagonal(factor, k, size) for k in range(2 * MOST)}
+    arrive(chunks - 2, range(MOST))
 
     for slot in range(MOST):
+        arrive(chunks - 1, (slot,))
         used = jnp.where(places == me * MOST + slot, F32(1), F32(0))
         active = jnp.max(used, axis=1, keepdims=True) > 0.5
+        energy_in = sum(energies[slot])
         precondition(
-            slot, active, shape, blocks, flipped, factor, (left_new, right_new), b, u, v, w, m, wide, ready
+            slot, active, tile, lanes, energy_in, tops, blocks, flipped, sums, factor, (left_new, right_new),
+            b, u, v, w, m, wide, ready,
         )
 
-        def give(k, carry):
-            o = partner(k)
+        for hop in HOPS:
+            o = partner(hop)
             pltpu.make_async_remote_copy(
                 src_ref=ready.at[slot, pl.ds(pl.multiple_of(o * stripe, stripe), stripe)],
                 dst_ref=back.at[me * MOST + slot],
@@ -338,9 +387,6 @@
                 device_id=(row, o),
                 device_id_type=MESH,
             ).start()
-            return carry
-
-        lax.fori_loop(1, count, give, 0)
         back[me * MOST + slot] = ready[slot, own_rows]
 
     for c in range(chunks):
@@ -362,7 +408,7 @@
     lax.fori_loop(0, count, put, 0)
 
 
-def whole_step(owner_table, grads, left, right, n_dp, lanes, shape):
+def whole_step(owner_table, grads, left, right, n_dp, lanes, tile):
     _, _, count, stripe, size = grads.shape
     chunks = size // lanes
     part = pltpu.VMEM((2, chunks, count // 2, stripe, lanes), BF16)
@@ -372,7 +418,7 @@
     DMA = pltpu.SemaphoreType.DMA
     hbm, vmem = pl.BlockSpec(memory_space=pltpu.HBM), pl.BlockSpec(memory_space=pltpu.VMEM)
     return pl.pallas_call(
-        functools.partial(step_kernel, n_dp, count, lanes, shape),
+        functools.partial(step_kernel, n_dp, count, lanes, tile),
         name="shampoo_step",
         out_shape=(
             jax.ShapeDtypeStruct((count, stripe, size), BF16),
@@ -394,6 +440,7 @@
             pltpu.VMEM((chunks, count, MOST, stripe, lanes), BF16),
             pair, pair,
             pltpu.VMEM((2 * MOST, size, size), F32),
+            pltpu.VMEM((2 * MOST, size, size), F32),
             thin, thin, thin, thin, thin,
             pltpu.VMEM((size, size), F32),
             pair,
@@ -409,7 +456,14 @@
 
 def store_kernel(*refs):
     sources, targets, sems = refs[:3], refs[3:6], refs[6]
-    copies = [pltpu.make_async_copy(s, t, sems.at[n]) for n, (s, t) in enumerate(zip(sources, targets))]
+    copies = []
+    for source, target in zip(sources, targets):
+        cuts = PIECES if source.shape[0] % PIECES == 0 else 1
+        step = source.shape[0] // cuts
+        rows = source.shape[1] // (PIECES // cuts)
+        for n in range(PIECES):
+            part = (pl.ds(n * step, step),) if cuts > 1 else (slice(None), pl.ds(n * rows, rows))
+            copies.append(pltpu.make_async_copy(source.at[part], target.at[part], sems.at[len(copies)]))
     for copy in copies:
         copy.start()
     for copy in copies:
@@ -423,13 +477,13 @@
         out_shape=tuple(jax.ShapeDtypeStruct(x.shape, x.dtype) for x in values),
         in_specs=[pl.BlockSpec(memory_space=pltpu.VMEM)] * 3,
         out_specs=tuple([pl.BlockSpec(memory_space=pltpu.HBM)] * 3),
-        scratch_shapes=[pltpu.SemaphoreType.DMA((3,))],
+        scratch_shapes=[pltpu.SemaphoreType.DMA((3 * PIECES,))],
         compiler_params=pltpu.CompilerParams(vmem_limit_bytes=8 * MIB),
     )(*values)
 
 
 def local(n_dp, grad_partial, owner_table, left_factor, right_factor):
-    values = whole_step(owner_table, grad_partial, left_factor, right_factor, n_dp, 128, (512, 256))
+    values = whole_step(owner_table, grad_partial, left_factor, right_factor, n_dp, 128, 256)
     update, new_left, new_right = store(*values)
     return update[None], new_left[None, None], new_right[None, None]
 

time: 62.5 us -> 58.9 us (0.942)
  Pallas kernels: 60.9 us -> 57.4 us
    pallas_call x1, Pallas kernels: 58.6 us -> 55.1 us  [whole_step(): pl.pallas_call(functools.partial(step_kernel, n_dp, count, lanes, tile),...]
where the time goes in v3:
time: 58.9 us; the launch traced here: 58.7 us
  Pallas kernels  57.4 us (97%)
  local copies, waits for them, and re-layouts  0.67 us (1%)
  between operations  0.65 us (1%)
    pallas_call x1, Pallas kernels, whole_step(): pl.pallas_call(functools.partial(step_kernel, n_dp, count, lanes, tile),...  55.1 us
    pallas_call x1, Pallas kernels, store(): pl.pallas_call(store_kernel, name='store', out_shape=tuple((jax.ShapeDtyp...  2.28 us

profile of v3, /device:TPU:1, one launch (start us, length us, event | category | flops | bytes accessed | tf_op | source)
XLA Modules:
  0.0 58.7 jit_solution(13130375251075059285)
XLA Ops:
  0.6 0.0 copy-start
  0.6 0.7 %copy-done = s32[4,32]{1,0:T(4,128)S(1)} copy-done((s32[4,32]{1,0:T(4,128)S(1)}, s32[4,32]{1,0:T(4,128)}, u32[]{:S(2)}) %copy-start) | copy-done | bytes 536
  1.3 55.1 %shampoo_step.1 = (bf16[32,16,512]{2,1,0:T(8,128)(2,1)S(1)}, f32[2,512,512]{2,1,0:T(8,128)S(1)}, f32[2,512,512]{2,1,0:T(8,128)S(1)}) custom-call(s32[4,32]{1,0:T(4,128)S(1)} %copy-done, f32[1,4,32,16,512]{4,3,2,1,0:T(8,128)} %grads.1, f32[1,1,2,512,512]{4,3,2,1,0:T(8,128)} %left.1, f32[1,1,2,512,512]{4,3,2,1,0:T(8,128)} %right.1), custom_call_target="tpu_custom_call" | custom-call | tf_op jit(solution)/shard_map/shampoo_step/pallas_call | solution.py:420
  56.5 2.3 %store.1 = (bf16[32,16,512]{2,1,0:T(8,128)(2,1)}, f32[2,512,512]{2,1,0:T(8,128)}, f32[2,512,512]{2,1,0:T(8,128)}) custom-call(bf16[32,16,512]{2,1,0:T(8,128)(2,1)S(1)} %get-tuple-element.9.refs_0_, f32[2,512,512]{2,1,0:T(8,128)S(1)} %get-tuple-element.10.refs_1_, f32[2,512,512]{2,1,0:T(8,128)S(1)} %get-tuple-element.11.refs_2_), custom_call_target="tpu_custom_call" | custom-call | tf_op jit(solution)/shard_map/store/pallas_call | solution.py:474
Async XLA Ops:
  0.6 0.7 %copy-start = (s32[4,32]{1,0:T(4,128)S(1)}, s32[4,32]{1,0:T(4,128)}, u32[]{:S(2)}) copy-start(s32[4,32]{1,0:T(4,128)} %owner_table.1) | copy-start | bytes 1540

commit v4 on v3

--- a/solution.py
+++ b/solution.py
@@ -20,6 +20,7 @@
     ((z, y, core) for z in range(SIDE) for y in range(SIDE) for core in range(2) if (z, y, core) != (0, 0, 0)),
     key=lambda hop: (-distance(hop), (hop[0] + hop[1]) % 2, hop),
 )
+CHIP_HOPS = [hop for hop in HOPS if hop[2] == 0]
 MESH = pl.DeviceIdType.MESH
 F32 = jnp.float32
 BF16 = jnp.bfloat16
@@ -86,7 +87,18 @@
     return energy
 
 
-def precondition(slot, active, tile, lanes, energy_in, tops, blocks, flipped, sums, factor, fresh, b, u, v, w, m, wide, result):
+def renew(slot, active, lanes, blocks, flipped, sums, factor, fresh):
+    size = blocks.shape[-1]
+    keep = jnp.where(active, F32(decay_rate), F32(1.0))
+    add = jnp.where(active, F32((1.0 - decay_rate) / size), F32(0.0))
+    final = pl.ds(size - lanes, lanes)
+    one, two = 2 * slot, 2 * slot + 1
+    product = sums[one] + dot(blocks[slot, :, final], flipped[slot, final, :])
+    fresh[0][slot] = keep * factor[one] + add * product
+    fresh[1][slot] = keep * factor[two] + add * sums[two]
+
+
+def precondition(slot, tile, lanes, energy_in, tops, blocks, flipped, sums, factor, b, u, v, w, m, wide, result):
     size = blocks.shape[-1]
     chains = (2 * slot, 2 * slot + 1)
     offsets = range(0, size, tile)
@@ -95,16 +107,13 @@
     tops = {k: tops[k] + grown for k in chains}
     shrink = {k: 1.0 / tops[k] for k in chains}
     columns_sum = {k: {} for k in chains}
-    keep = jnp.where(active, F32(decay_rate), F32(1.0))
-    add = jnp.where(active, F32((1.0 - decay_rate) / size), F32(0.0))
 
     def gram(k, i, j, rows, columns):
         product = sums[k, rows, columns]
         if k % 2 == 0:
             final = pl.ds(size - lanes, lanes)
             product += dot(blocks[slot, rows, final], flipped[slot, final, columns])
-        new = keep * factor[k, rows, columns] + add * product
-        fresh[k % 2][slot, rows, columns] = new
+        new = decay_rate * factor[k, rows, columns] + ((1.0 - decay_rate) / size) * product
         value = plus_diagonal(new * shrink[k], i, j, damping * shrink[k])
         b[k, rows, columns] = value.astype(BF16)
         part = jnp.sum(value, axis=0, keepdims=True)
@@ -138,17 +147,16 @@
     vector = {
         k: jnp.concatenate([columns_sum[k][j] for j in sorted(columns_sum[k])], axis=1) for k in chains
     }
-    length = {}
+    squares = {}
     for matrix in (w, w, b):
+        lines = dict(vector)
         for k in chains:
-            vector[k] = vector[k] * lax.rsqrt(jnp.sum(vector[k] * vector[k], axis=1, keepdims=True))
-        for k in chains:
-            high = vector[k].astype(BF16)
-            low = (vector[k] - high.astype(F32)).astype(BF16)
+            high = lines[k].astype(BF16)
+            low = (lines[k] - high.astype(F32)).astype(BF16)
             both = dot(jnp.concatenate([high, low], axis=0), matrix[k])
-            vector[k] = both[0:1] + both[1:2]
-    for k in chains:
-        length[k] = jnp.sqrt(jnp.sum(vector[k] * vector[k], axis=1, keepdims=True))
+            squares[k] = jnp.sum(lines[k] * lines[k], axis=1, keepdims=True)
+            vector[k] = (both[0:1] + both[1:2]) * lax.rsqrt(squares[k])
+    length = {k: jnp.sqrt(jnp.sum(vector[k] * vector[k], axis=1, keepdims=True)) for k in chains}
     c1 = {k: 1.0 / (1.25 * length[k]) for k in chains}
     c2 = {k: c1[k] * c1[k] for k in chains}
     c3 = {k: c2[k] * c1[k] for k in chains}
@@ -202,14 +210,14 @@
         wide[:, columns] = shaped
         energy += whole_sum(shaped * shaped)
     graft = jnp.sqrt(energy_in / (size * size)) / jnp.sqrt(energy / (size * size) + epsilon)
-    result[slot] = (wide[...] * graft).astype(BF16)
+    result[slot] = (wide[...] * graft).astype(BF16).reshape(result.shape[1:])
 
 
 def step_kernel(
     n_dp, count, lanes, tile, owner_table, grads, left, right, update, left_new, right_new, owners_v, owners_s,
     place_v, place_s, block_v, block_s, stage, raw, raw_in, cross, cross_in, both, both_in, summed, outgoing,
     blocks, flipped, sums, factor, b, u, v, w, m, wide, ready, back, load_sem, factor_sem, table_sem, x_send, x_recv,
-    o_send, o_recv, r_send, r_recv,
+    o_send, o_recv, r_send, r_recv, hand_sem,
 ):
     row, me = lax.axis_index("dp"), lax.axis_index("block")
     stripe = grads.shape[3]
@@ -234,11 +242,12 @@
         load.start()
 
     my_chip, my_core = (me // (2 * SIDE), lax.rem(me // 2, SIDE)), lax.rem(me, 2)
+    chip = me // 2
 
     def partner(hop):
         z, y, core = hop
-        chip = lax.rem(my_chip[0] + z, SIDE) * SIDE + lax.rem(my_chip[1] + y, SIDE)
-        return chip * 2 + lax.rem(my_core + core, 2)
+        there = lax.rem(my_chip[0] + z, SIDE) * SIDE + lax.rem(my_chip[1] + y, SIDE)
+        return there * 2 + lax.rem(my_core + core, 2)
 
     barrier = pltpu.get_barrier_semaphore()
     for peer in (near, behind):
@@ -369,25 +378,52 @@
 
     for slot in range(MOST):
         arrive(chunks - 1, (slot,))
+        energy_in = sum(energies[slot])
+        precondition(
+            slot, tile, lanes, energy_in, tops, blocks, flipped, sums, factor, b, u, v, w, m, wide, ready
+        )
+
+        if slot == 0:
+            for hop in CHIP_HOPS:
+                o = partner(hop)
+                pltpu.make_async_remote_copy(
+                    src_ref=ready.at[0, pl.ds(o - my_core, 2)],
+                    dst_ref=back.at[pl.ds(0, 2), chip],
+                    send_sem=r_send.at[0],
+                    recv_sem=r_recv.at[0],
+                    device_id=(row, o),
+                    device_id_type=MESH,
+                ).start()
+            for core in range(2):
+                back[core, chip] = ready[0, me - my_core + core]
+        else:
+            for hop in HOPS:
+                o = partner(hop)
+                pltpu.make_async_remote_copy(
+                    src_ref=ready.at[1, o],
+                    dst_ref=back.at[3 + my_core, chip],
+                    send_sem=r_send.at[1],
+                    recv_sem=r_recv.at[1],
+                    device_id=(row, o),
+                    device_id_type=MESH,
+                ).start()
+            back[3 + my_core, chip] = ready[1, me]
+
+    chip_pairs = ready.at[0, pl.ds(0, count - 2)]
+    pltpu.make_async_copy(chip_pairs, chip_pairs, r_recv.at[0]).wait()
+    hand_over = pltpu.make_async_remote_copy(
+        src_ref=back.at[1 - my_core],
+        dst_ref=back.at[2],
+        send_sem=hand_sem.at[0],
+        recv_sem=hand_sem.at[1],
+        device_id=(row, partner((0, 0, 1))),
+        device_id_type=MESH,
+    )
+    hand_over.start()
+    for slot in range(MOST):
         used = jnp.where(places == me * MOST + slot, F32(1), F32(0))
         active = jnp.max(used, axis=1, keepdims=True) > 0.5
-        energy_in = sum(energies[slot])
-        precondition(
-            slot, active, tile, lanes, energy_in, tops, blocks, flipped, sums, factor, (left_new, right_new),
-            b, u, v, w, m, wide, ready,
-        )
-
-        for hop in HOPS:
-            o = partner(hop)
-            pltpu.make_async_remote_copy(
-                src_ref=ready.at[slot, pl.ds(pl.multiple_of(o * stripe, stripe), stripe)],
-                dst_ref=back.at[me * MOST + slot],
-                send_sem=r_send.at[slot],
-                recv_sem=r_recv.at[slot],
-                device_id=(row, o),
-                device_id_type=MESH,
-            ).start()
-        back[me * MOST + slot] = ready[slot, own_rows]
+        renew(slot, active, lanes, blocks, flipped, sums, factor, (left_new, right_new))
 
     for c in range(chunks):
         for way in range(2):
@@ -396,13 +432,18 @@
             boths[c][way].wait_send()
         arrived = outgoing.at[c, pl.ds(0, count - 1)]
         pltpu.make_async_copy(arrived, arrived, o_send.at[c]).wait()
-    for slot in range(MOST):
-        arrived = back.at[pl.ds(0, count - 1)]
-        pltpu.make_async_copy(arrived, arrived, r_recv.at[slot]).wait()
-        pltpu.make_async_copy(arrived, arrived, r_send.at[slot]).wait()
+    pltpu.make_async_copy(chip_pairs, chip_pairs, r_send.at[0]).wait()
+    hand_over.wait()
+    others = ready.at[1, pl.ds(0, count - 1)]
+    pltpu.make_async_copy(others, others, r_send.at[1]).wait()
+    pltpu.make_async_copy(others, others, r_recv.at[1]).wait()
 
     def put(j, carry):
-        update[j] = back[place_s[0, j]]
+        place = place_s[0, j]
+        owner, slot = place // MOST, lax.rem(place, MOST)
+        owner_chip, owner_core = owner // 2, lax.rem(owner, 2)
+        plane = jnp.where(slot == 0, jnp.where(owner_core == my_core, my_core, 2), 3 + owner_core)
+        update[j] = back[plane, owner_chip]
         return carry
 
     lax.fori_loop(0, count, put, 0)
@@ -443,10 +484,10 @@
             pltpu.VMEM((2 * MOST, size, size), F32),
             thin, thin, thin, thin, thin,
             pltpu.VMEM((size, size), F32),
-            pair,
-            pltpu.VMEM((MOST * count, stripe, size), BF16),
+            pltpu.VMEM((MOST, count, stripe, size), BF16),
+            pltpu.VMEM((5, count // 2, stripe, size), BF16),
             DMA((4,)), DMA((2 * MOST,)), DMA((4,)), DMA((3, 2, chunks)), DMA((3, 2, chunks)),
-            DMA((chunks,)), DMA((chunks,)), DMA((MOST,)), DMA((MOST,)),
+            DMA((chunks,)), DMA((chunks,)), DMA((MOST,)), DMA((MOST,)), DMA((2,)),
         ],
         compiler_params=pltpu.CompilerParams(
             collective_id=0, has_side_effects=True, vmem_limit_bytes=48 * MIB
@@ -483,6 +524,7 @@
 
 
 def local(n_dp, grad_partial, owner_table, left_factor, right_factor):
+    owner_table = pltpu.with_memory_space_constraint(owner_table, pltpu.HBM)
     values = whole_step(owner_table, grad_partial, left_factor, right_factor, n_dp, 128, 256)
     update, new_left, new_right = store(*values)
     return update[None], new_left[None, None], new_right[None, None]

time: 58.9 us -> 58.1 us (0.986)
  local copies, waits for them, and re-layouts: 0.67 us -> 0 us
    unnamed x2 -> x0, local copies, waits for them, and re-layouts: 0.67 us -> none
where the time goes in v4:
time: 58.1 us; the launch traced here: 58 us
  Pallas kernels  57.2 us (98%)
  between operations  0.8 us (1%)
    pallas_call x1, Pallas kernels, whole_step(): pl.pallas_call(functools.partial(step_kernel, n_dp, count, lanes, tile),...  54.9 us
    pallas_call x1, Pallas kernels, store(): pl.pallas_call(store_kernel, name='store', out_shape=tuple((jax.ShapeDtyp...  2.28 us

profile of v4, /device:TPU:1, one launch (start us, length us, event | category | flops | bytes accessed | tf_op | source)
XLA Modules:
  0.0 58.0 jit_solution(12379957845491396063)
XLA Ops:
  0.6 54.9 %shampoo_step.1 = (bf16[32,16,512]{2,1,0:T(8,128)(2,1)S(1)}, f32[2,512,512]{2,1,0:T(8,128)S(1)}, f32[2,512,512]{2,1,0:T(8,128)S(1)}) custom-call(s32[4,32]{1,0:T(4,128)} %owner_table.1, f32[1,4,32,16,512]{4,3,2,1,0:T(8,128)} %grads.1, f32[1,1,2,512,512]{4,3,2,1,0:T(8,128)} %left.1, f32[1,1,2,512,512]{4,3,2,1,0:T(8,128)} %right.1), custom_call_target="tpu_custom_call" | custom-call | tf_op jit(solution)/shard_map/shampoo_step/pallas_call | solution.py:461
  55.5 2.3 %store.1 = (bf16[32,16,512]{2,1,0:T(8,128)(2,1)}, f32[2,512,512]{2,1,0:T(8,128)}, f32[2,512,512]{2,1,0:T(8,128)}) custom-call(bf16[32,16,512]{2,1,0:T(8,128)(2,1)S(1)} %get-tuple-element.9.refs_0_, f32[2,512,512]{2,1,0:T(8,128)S(1)} %get-tuple-element.10.refs_1_, f32[2,512,512]{2,1,0:T(8,128)S(1)} %get-tuple-element.11.refs_2_), custom_call_target="tpu_custom_call" | custom-call | tf_op jit(solution)/shard_map/store/pallas_call | solution.py:515

commit v5 on v4

--- a/solution.py
+++ b/solution.py
@@ -26,6 +26,7 @@
 BF16 = jnp.bfloat16
 MIB = 1 << 20
 PIECES = 4
+PER_ROUND = 2
 
 decay_rate = 0.9
 damping = 0.1
@@ -224,6 +225,7 @@
     half = count // 2
     size = grads.shape[4]
     chunks = size // lanes
+    rounds, broad = chunks // PER_ROUND, lanes * PER_ROUND
     near, behind, far = lax.rem(row + 1, n_dp), lax.rem(row + n_dp - 1, n_dp), lax.rem(row + 2, n_dp)
 
     table_loads = [
@@ -277,29 +279,31 @@
     crosses = [[x_copy(1, way, c, cross, cross_in) for way in range(2)] for c in range(chunks)]
     boths = [[x_copy(2, way, c, both, both_in) for way in range(2)] for c in range(chunks)]
 
-    def dispatch(c):
-        columns = pl.ds(c * lanes, lanes)
+    def reduce(c):
+        r, columns = c // PER_ROUND, pl.ds((c % PER_ROUND) * lanes, lanes)
         for way in range(2):
             crosses[c][way].wait_recv()
             boths[c][way].wait_recv()
         for part in range(2):
             total = cut(3, part, c) + both_in[part, c].astype(F32) + cross_in[1 - part, c].astype(F32)
-            summed[c, halves[part]] = total.astype(BF16)
-
+            summed[r, halves[part], :, columns] = total.astype(BF16)
+
+    def dispatch(r):
+        for o in range(count):
+            for s in range(MOST):
+                outgoing[r, o, s] = summed[r, block_s[0, o * MOST + s]]
+        columns = pl.ds(r * broad, broad)
         for hop in HOPS:
             o = partner(hop)
-            for s in range(MOST):
-                outgoing[c, o, s] = summed[c, block_s[0, o * MOST + s]]
             pltpu.make_async_remote_copy(
-                src_ref=outgoing.at[c, o],
+                src_ref=outgoing.at[r, o],
                 dst_ref=blocks.at[:, own_rows, columns],
-                send_sem=o_send.at[c],
-                recv_sem=o_recv.at[c],
+                send_sem=o_send.at[r],
+                recv_sem=o_recv.at[r],
                 device_id=(row, o),
                 device_id_type=MESH,
             ).start()
-        for s in range(MOST):
-            blocks[s, own_rows, columns] = summed[c, block_s[0, me * MOST + s]]
+        blocks[:, own_rows, columns] = outgoing[r, me]
 
     def start_raw(c):
         for way in range(2):
@@ -316,12 +320,12 @@
 
     energies = [[] for _ in range(MOST)]
 
-    def arrive(c, slots_here):
-        if slots_here[0] == 0:
-            arrived = outgoing.at[c, pl.ds(0, count - 1)]
-            pltpu.make_async_copy(arrived, arrived, o_recv.at[c]).wait()
-        for slot in slots_here:
-            energies[slot].append(absorb(slot, c, lanes, blocks, flipped, sums, c == chunks - 1))
+    def arrive(r):
+        arrived = outgoing.at[r, pl.ds(0, count - 1)]
+        pltpu.make_async_copy(arrived, arrived, o_recv.at[r]).wait()
+
+    def take(r, slot):
+        energies[slot].append(absorb(slot, r, broad, blocks, flipped, sums, r == rounds - 1))
 
     loads[0].wait()
     start_raw(0)
@@ -329,6 +333,7 @@
     loads[2].wait()
     start_cross(0)
     start_raw(1)
+    start_cross(1)
 
     for load in table_loads:
         load.wait()
@@ -358,29 +363,31 @@
         load.start()
 
     for c in range(chunks):
-        if c > 0:
-            start_cross(c)
-            if c + 1 < chunks:
-                start_raw(c + 1)
         for way in range(2):
             raws[c][way].wait_recv()
             both[way, c] = (cut(1 + way, way, c) + raw_in[way, c].astype(F32)).astype(BF16)
             boths[c][way].start()
-        if c > 0:
-            dispatch(c - 1)
-        if c > 1:
-            arrive(c - 2, range(MOST))
-    dispatch(chunks - 1)
+        if c + 2 < chunks:
+            start_raw(c + 2)
+            start_cross(c + 2)
+    for r in range(rounds):
+        for c in range(r * PER_ROUND, (r + 1) * PER_ROUND):
+            reduce(c)
+        dispatch(r)
     for load in factor_loads:
         load.wait()
     tops = {k: decay_rate * largest_diagonal(factor, k, size) for k in range(2 * MOST)}
-    arrive(chunks - 2, range(MOST))
+    for r in range(rounds - 1):
+        arrive(r)
+        for slot in range(MOST):
+            take(r, slot)
+    arrive(rounds - 1)
 
     for slot in range(MOST):
-        arrive(chunks - 1, (slot,))
+        take(rounds - 1, slot)
         energy_in = sum(energies[slot])
         precondition(
-            slot, tile, lanes, energy_in, tops, blocks, flipped, sums, factor, b, u, v, w, m, wide, ready
+            slot, tile, broad, energy_in, tops, blocks, flipped, sums, factor, b, u, v, w, m, wide, ready
         )
 
         if slot == 0:
@@ -423,35 +430,34 @@
     for slot in range(MOST):
         used = jnp.where(places == me * MOST + slot, F32(1), F32(0))
         active = jnp.max(used, axis=1, keepdims=True) > 0.5
-        renew(slot, active, lanes, blocks, flipped, sums, factor, (left_new, right_new))
+        renew(slot, active, broad, blocks, flipped, sums, factor, (left_new, right_new))
 
     for c in range(chunks):
         for way in range(2):
             raws[c][way].wait_send()
             crosses[c][way].wait_send()
             boths[c][way].wait_send()
-        arrived = outgoing.at[c, pl.ds(0, count - 1)]
-        pltpu.make_async_copy(arrived, arrived, o_send.at[c]).wait()
+    for r in range(rounds):
+        arrived = outgoing.at[r, pl.ds(0, count - 1)]
+        pltpu.make_async_copy(arrived, arrived, o_send.at[r]).wait()
     pltpu.make_async_copy(chip_pairs, chip_pairs, r_send.at[0]).wait()
     hand_over.wait()
     others = ready.at[1, pl.ds(0, count - 1)]
     pltpu.make_async_copy(others, others, r_send.at[1]).wait()
     pltpu.make_async_copy(others, others, r_recv.at[1]).wait()
 
-    def put(j, carry):
+    for j in range(count):
         place = place_s[0, j]
         owner, slot = place // MOST, lax.rem(place, MOST)
         owner_chip, owner_core = owner // 2, lax.rem(owner, 2)
         plane = jnp.where(slot == 0, jnp.where(owner_core == my_core, my_core, 2), 3 + owner_core)
         update[j] = back[plane, owner_chip]
-        return carry
-
-    lax.fori_loop(0, count, put, 0)
 
 
 def whole_step(owner_table, grads, left, right, n_dp, lanes, tile):
     _, _, count, stripe, size = grads.shape
     chunks = size // lanes
+    rounds = chunks // PER_ROUND
     part = pltpu.VMEM((2, chunks, count // 2, stripe, lanes), BF16)
     thin = pltpu.VMEM((2 * MOST, size, size), BF16)
     pair = pltpu.VMEM((MOST, size, size), BF16)
@@ -477,8 +483,8 @@
             pltpu.SMEM((1, slots), jnp.int32),
             pltpu.VMEM((4, count, stripe, size), F32),
             part, part, part, part, part, part,
-            pltpu.VMEM((chunks, count, stripe, lanes), BF16),
-            pltpu.VMEM((chunks, count, MOST, stripe, lanes), BF16),
+            pltpu.VMEM((rounds, count, stripe, PER_ROUND * lanes), BF16),
+            pltpu.VMEM((rounds, count, MOST, stripe, PER_ROUND * lanes), BF16),
             pair, pair,
             pltpu.VMEM((2 * MOST, size, size), F32),
             pltpu.VMEM((2 * MOST, size, size), F32),
@@ -487,7 +493,7 @@
             pltpu.VMEM((MOST, count, stripe, size), BF16),
             pltpu.VMEM((5, count // 2, stripe, size), BF16),
             DMA((4,)), DMA((2 * MOST,)), DMA((4,)), DMA((3, 2, chunks)), DMA((3, 2, chunks)),
-            DMA((chunks,)), DMA((chunks,)), DMA((MOST,)), DMA((MOST,)), DMA((2,)),
+            DMA((rounds,)), DMA((rounds,)), DMA((MOST,)), DMA((MOST,)), DMA((2,)),
         ],
         compiler_params=pltpu.CompilerParams(
             collective_id=0, has_side_effects=True, vmem_limit_bytes=48 * MIB

time: 58.1 us -> 61.3 us (1.055)
  Pallas kernels: 57.2 us -> 60.6 us
    pallas_call x1, Pallas kernels: 54.9 us -> 58.3 us  [whole_step(): pl.pallas_call(functools.partial(step_kernel, n_dp, count, lanes, tile),...]
where the time goes in v5:
time: 61.3 us; the launch traced here: 61.2 us
  Pallas kernels  60.6 us (99%)
  between operations  0.64 us (1%)
    pallas_call x1, Pallas kernels, whole_step(): pl.pallas_call(functools.partial(step_kernel, n_dp, count, lanes, tile),...  58.3 us
    pallas_call x1, Pallas kernels, store(): pl.pallas_call(store_kernel, name='store', out_shape=tuple((jax.ShapeDtyp...  2.28 us

profile of v5, /device:TPU:1, one launch (start us, length us, event | category | flops | bytes accessed | tf_op | source)
XLA Modules:
  0.0 61.2 jit_solution(11839963218893345353)
XLA Ops:
  0.6 58.3 %shampoo_step.1 = (bf16[32,16,512]{2,1,0:T(8,128)(2,1)S(1)}, f32[2,512,512]{2,1,0:T(8,128)S(1)}, f32[2,512,512]{2,1,0:T(8,128)S(1)}) custom-call(s32[4,32]{1,0:T(4,128)} %owner_table.1, f32[1,4,32,16,512]{4,3,2,1,0:T(8,128)} %grads.1, f32[1,1,2,512,512]{4,3,2,1,0:T(8,128)} %left.1, f32[1,1,2,512,512]{4,3,2,1,0:T(8,128)} %right.1), custom_call_target="tpu_custom_call" | custom-call | tf_op jit(solution)/shard_map/shampoo_step/pallas_call | solution.py:467
  58.9 2.3 %store.1 = (bf16[32,16,512]{2,1,0:T(8,128)(2,1)}, f32[2,512,512]{2,1,0:T(8,128)}, f32[2,512,512]{2,1,0:T(8,128)}) custom-call(bf16[32,16,512]{2,1,0:T(8,128)(2,1)S(1)} %get-tuple-element.9.refs_0_, f32[2,512,512]{2,1,0:T(8,128)S(1)} %get-tuple-element.10.refs_1_, f32[2,512,512]{2,1,0:T(8,128)S(1)} %get-tuple-element.11.refs_2_), custom_call_target="tpu_custom_call" | custom-call | tf_op jit(solution)/shard_map/store/pallas_call | solution.py:521

commit v6 on v4

--- a/solution.py
+++ b/solution.py
@@ -116,8 +116,6 @@
         new = decay_rate * factor[k, rows, columns] + ((1.0 - decay_rate) / size) * product
         value = plus_diagonal(new * shrink[k], i, j, damping * shrink[k])
         b[k, rows, columns] = value.astype(BF16)
-        part = jnp.sum(value, axis=0, keepdims=True)
-        columns_sum[k][j] = columns_sum[k][j] + part if j in columns_sum[k] else part
 
     for k in chains:
         for j in offsets:
@@ -138,8 +136,16 @@
     def square(k, i, j, rows, columns):
         return (dot(b[k, rows, :], b[k, :, columns]).astype(BF16),)
 
+    def count_in(k, j, value):
+        part = jnp.sum(value.astype(F32), axis=0, keepdims=True)
+        columns_sum[k][j] = columns_sum[k][j] + part if j in columns_sum[k] else part
+
     def cube(k, i, j, rows, columns):
-        return (dot(b[k, rows, :], u[k, :, columns]).astype(BF16),)
+        value = dot(b[k, rows, :], u[k, :, columns]).astype(BF16)
+        count_in(k, j, value)
+        if i != j:
+            count_in(k, i, value.T)
+        return (value,)
 
     each(square, u)
     each(cube, w)
@@ -147,16 +153,18 @@
     vector = {
         k: jnp.concatenate([columns_sum[k][j] for j in sorted(columns_sum[k])], axis=1) for k in chains
     }
-    squares = {}
-    for matrix in (w, w, b):
-        lines = dict(vector)
-        for k in chains:
-            high = lines[k].astype(BF16)
-            low = (lines[k] - high.astype(F32)).astype(BF16)
-            both = dot(jnp.concatenate([high, low], axis=0), matrix[k])
-            squares[k] = jnp.sum(lines[k] * lines[k], axis=1, keepdims=True)
-            vector[k] = (both[0:1] + both[1:2]) * lax.rsqrt(squares[k])
-    length = {k: jnp.sqrt(jnp.sum(vector[k] * vector[k], axis=1, keepdims=True)) for k in chains}
+    def times(matrix, k, line):
+        high = line.astype(BF16)
+        low = (line - high.astype(F32)).astype(BF16)
+        both = dot(jnp.concatenate([high, low], axis=0), matrix[k])
+        return both[0:1] + both[1:2]
+
+    def inner(one, two):
+        return jnp.sum(one * two, axis=1, keepdims=True)
+
+    q = {k: times(w, k, vector[k]) * lax.rsqrt(inner(vector[k], vector[k])) for k in chains}
+    r = {k: times(u, k, q[k]) for k in chains}
+    length = {k: jnp.sqrt(inner(r[k], r[k]) / inner(q[k], r[k])) for k in chains}
     c1 = {k: 1.0 / (1.25 * length[k]) for k in chains}
     c2 = {k: c1[k] * c1[k] for k in chains}
     c3 = {k: c2[k] * c1[k] for k in chains}
@@ -438,15 +446,12 @@
     pltpu.make_async_copy(others, others, r_send.at[1]).wait()
     pltpu.make_async_copy(others, others, r_recv.at[1]).wait()
 
-    def put(j, carry):
+    for j in range(count):
         place = place_s[0, j]
         owner, slot = place // MOST, lax.rem(place, MOST)
         owner_chip, owner_core = owner // 2, lax.rem(owner, 2)
         plane = jnp.where(slot == 0, jnp.where(owner_core == my_core, my_core, 2), 3 + owner_core)
         update[j] = back[plane, owner_chip]
-        return carry
-
-    lax.fori_loop(0, count, put, 0)
 
 
 def whole_step(owner_table, grads, left, right, n_dp, lanes, tile):

time: 58.1 us -> 57.4 us (0.988)
  Pallas kernels: 57.2 us -> 56.5 us
    pallas_call x1, Pallas kernels: 54.9 us -> 54.2 us  [whole_step(): pl.pallas_call(functools.partial(step_kernel, n_dp, count, lanes, tile),...]
where the time goes in v6:
time: 57.4 us; the launch traced here: 57.3 us
  Pallas kernels  56.5 us (98%)
  between operations  0.8 us (1%)
    pallas_call x1, Pallas kernels, whole_step(): pl.pallas_call(functools.partial(step_kernel, n_dp, count, lanes, tile),...  54.2 us
    pallas_call x1, Pallas kernels, store(): pl.pallas_call(store_kernel, name='store', out_shape=tuple((jax.ShapeDtyp...  2.28 us

profile of v6, /device:TPU:1, one launch (start us, length us, event | category | flops | bytes accessed | tf_op | source)
XLA Modules:
  0.0 57.3 jit_solution(12065385038867131000)
XLA Ops:
  0.6 54.2 %shampoo_step.1 = (bf16[32,16,512]{2,1,0:T(8,128)(2,1)S(1)}, f32[2,512,512]{2,1,0:T(8,128)S(1)}, f32[2,512,512]{2,1,0:T(8,128)S(1)}) custom-call(s32[4,32]{1,0:T(4,128)} %owner_table.1, f32[1,4,32,16,512]{4,3,2,1,0:T(8,128)} %grads.1, f32[1,1,2,512,512]{4,3,2,1,0:T(8,128)} %left.1, f32[1,1,2,512,512]{4,3,2,1,0:T(8,128)} %right.1), custom_call_target="tpu_custom_call" | custom-call | tf_op jit(solution)/shard_map/shampoo_step/pallas_call | solution.py:466
  54.9 2.3 %store.1 = (bf16[32,16,512]{2,1,0:T(8,128)(2,1)}, f32[2,512,512]{2,1,0:T(8,128)}, f32[2,512,512]{2,1,0:T(8,128)}) custom-call(bf16[32,16,512]{2,1,0:T(8,128)(2,1)S(1)} %get-tuple-element.9.refs_0_, f32[2,512,512]{2,1,0:T(8,128)S(1)} %get-tuple-element.10.refs_1_, f32[2,512,512]{2,1,0:T(8,128)S(1)} %get-tuple-element.11.refs_2_), custom_call_target="tpu_custom_call" | custom-call | tf_op jit(solution)/shard_map/store/pallas_call | solution.py:520
